TPU v7x, 256 devices: a whole 4x4x8 slice. The times are simulated.
256 devices in a mesh: row: 32 (over x_hi, z, core), col: 8 (over y, x_lo).
Axes of the slice: x: 4 (x_hi: 2, x_lo: 2; x = x_hi * 2 + x_lo), y: 4, z: 8, core: 2. Of those that a mesh axis runs over, the one named last changes fastest.
Arguments:
- object_field: float32 [2, 2, 8192, 2048], P(None, None, 'row', 'col'), may hold values from -4 to 4
- probe_wave: float32 [2, 256, 256], replicated, may hold values from -6 to 6
- positions: int32 [32, 8, 6, 2], P('row', 'col'), may hold values from 0 to 256, as said below
- counts: int32 [32, 8], P('row', 'col'), may hold values from 1 to 6, as said below
- amplitudes: bfloat16 [32, 8, 6, 256, 256], P('row', 'col'), may hold values from 0 to 3
Outputs:
- updated_object: float32 [2, 2, 8192, 2048], P(None, None, 'row', 'col')
Inputs may be any that keep to these rules, and one draw needn't show every extreme that they name: `positions`: the window of a slot covers 256 x 256 pixels of a frame that begins 128 pixels above and left of its tile. Slots at and after the tile's count are unused. `counts`: some tile uses all 6 slots in every draw.
All inputs are finite; a program needn't handle non-finite values.
Results may differ from a plain program's by a relative error of at most 0.024.
Values may be sent and summed in bfloat16 or wider, within the bound.
No kernel may reach another device: no remote copies, remote signals or barrier semaphores. Data moves between devices by JAX's collectives and lax.ppermute only.
A program may use at most 64 MiB of HBM per device.

v0:
```python
import jax
import jax.numpy as jnp
from jax import lax
from jax.sharding import PartitionSpec as P

ITERS = 2


smooth_floor = 0.25
descent_rate = 0.1


def passed_along(value, axis, steps):
    count = lax.axis_size(axis)
    leading, last = (max(0, -steps), min(count, count - steps))
    return lax.ppermute(value, axis, [(source, source + steps) for source in range(leading, last)])


def padded(cells, sides, width):
    for axis, dim in sides:
        count = lax.axis_size(axis)
        ends = count - 1
        head = lax.slice_in_dim(cells, 0, width, axis=dim)
        tail = lax.slice_in_dim(cells, cells.shape[dim] - width, cells.shape[dim], axis=dim)
        cells = jnp.concatenate(
            [
                lax.ppermute(tail, axis, [(i, (i + 1) % count) for i in range(ends)]),
                cells,
                lax.ppermute(head, axis, [((i + 1) % count, i) for i in range(ends)]),
            ],
            axis=dim,
        )
    return cells


def make_tables(points):
    indices = jnp.arange(points, dtype=jnp.int32)
    products = indices[:, None] * indices[None, :] % points
    phases = 2.0 * jnp.pi / points * products.astype(jnp.float32)
    scaling = 1.0 / jnp.sqrt(jnp.float32(points))
    cosines = jnp.cos(phases)
    sine_table = jnp.sin(phases)
    fourier = (
        (cosines * scaling).astype(jnp.bfloat16),
        (-sine_table * scaling).astype(jnp.bfloat16),
    )
    frequency = jnp.where(indices < points // 2, indices, indices - points).astype(jnp.float32)
    chirp_phase = -jnp.pi / (2.0 * points) * frequency * frequency
    chirp_cos = jnp.cos(chirp_phase)[None, :]
    chirp_sin = jnp.sin(chirp_phase)[None, :]
    highest = lax.Precision.HIGHEST
    cos_real = jnp.dot(cosines * chirp_cos, cosines, precision=highest)
    sin_real = jnp.dot(sine_table * chirp_cos, sine_table, precision=highest)
    sin_imag = jnp.dot(sine_table * chirp_sin, cosines, precision=highest)
    cos_imag = jnp.dot(cosines * chirp_sin, sine_table, precision=highest)
    mixed_one = jnp.dot(sine_table * chirp_cos, cosines, precision=highest)
    mixed_two = jnp.dot(cosines * chirp_cos, sine_table, precision=highest)
    plain_one = jnp.dot(cosines * chirp_sin, cosines, precision=highest)
    plain_two = jnp.dot(sine_table * chirp_sin, sine_table, precision=highest)
    kernel_real = (cos_real + sin_real - sin_imag + cos_imag) / points
    kernel_imaginary = (mixed_one - mixed_two + plain_one + plain_two) / points
    propagator = (kernel_real.astype(jnp.bfloat16), kernel_imaginary.astype(jnp.bfloat16))
    return (fourier, propagator)


def complex_product(left_factor, right_factor):
    return (
        left_factor[0] * right_factor[0] - left_factor[1] * right_factor[1],
        left_factor[0] * right_factor[1] + left_factor[1] * right_factor[0],
    )


def conjugate(operand):
    return (operand[0], -operand[1])


def to_half(operand):
    return (operand[0].astype(jnp.bfloat16), operand[1].astype(jnp.bfloat16))


def apply_left(matrix, operand):
    rows_count = matrix[0].shape[0]
    cols_count = operand[0].shape[1]
    stacked = jnp.concatenate([matrix[0], matrix[1]], axis=0)
    joined = jnp.concatenate([operand[0], operand[1]], axis=1)
    result = jnp.dot(stacked, joined, preferred_element_type=jnp.float32)
    return (
        result[:rows_count, :cols_count] - result[rows_count:, cols_count:],
        result[:rows_count, cols_count:] + result[rows_count:, :cols_count],
    )


def apply_right(operand, matrix):
    rows_count = operand[0].shape[0]
    cols_count = matrix[0].shape[1]
    stacked = jnp.concatenate([operand[0], operand[1]], axis=0)
    joined = jnp.concatenate([matrix[0], matrix[1]], axis=1)
    result = jnp.dot(stacked, joined, preferred_element_type=jnp.float32)
    return (
        result[:rows_count, :cols_count] - result[rows_count:, cols_count:],
        result[:rows_count, cols_count:] + result[rows_count:, :cols_count],
    )


def transform(matrix, operand):
    return apply_right(to_half(apply_left(matrix, operand)), matrix)


def slot_gradient(window, probe_field, measured, tables):
    fourier, propagator = tables
    layers = window.astype(jnp.float32)
    first_layer = (1.0 + layers[0, 0], layers[0, 1])
    second_layer = (1.0 + layers[1, 0], layers[1, 1])
    entrance = to_half(complex_product(probe_field, first_layer))
    middle = to_half(transform(propagator, entrance))
    middle_wide = (middle[0].astype(jnp.float32), middle[1].astype(jnp.float32))
    leaving = to_half(complex_product(middle_wide, second_layer))
    distant = transform(fourier, leaving)
    modulus = jnp.sqrt(distant[0] * distant[0] + distant[1] * distant[1] + smooth_floor)
    factor = 1.0 - measured.astype(jnp.float32) / modulus
    residual = to_half((factor * distant[0], factor * distant[1]))
    back_far = transform(conjugate(fourier), residual)
    back_middle = to_half(complex_product(back_far, conjugate(second_layer)))
    back_near = transform(conjugate(propagator), back_middle)
    first_grad = complex_product(back_near, conjugate(probe_field))
    second_grad = complex_product(back_far, conjugate(middle_wide))
    return jnp.stack([jnp.stack(first_grad), jnp.stack(second_grad)])


def window_at(source, corner, extent):
    anchor = jnp.zeros((), jnp.int32)
    return lax.dynamic_slice(source, (anchor, anchor, corner[0], corner[1]), (2, 2, extent, extent))


def add_window(accumulated, corner, update):
    extent = update.shape[-1]
    anchor = jnp.zeros((), jnp.int32)
    current = window_at(accumulated, corner, extent)
    return lax.dynamic_update_slice(
        accumulated, current + update, (anchor, anchor, corner[0], corner[1])
    )


def fold_rows(gradient, half_width):
    interior = gradient.shape[2] - 2 * half_width
    upper_rim = gradient[:, :, :half_width]
    lower_rim = gradient[:, :, interior + half_width :]
    middle = gradient[:, :, half_width : interior + half_width]
    from_below = passed_along(upper_rim.astype(jnp.bfloat16), "row", -1).astype(upper_rim.dtype)
    from_above = passed_along(lower_rim.astype(jnp.bfloat16), "row", 1).astype(lower_rim.dtype)
    middle = middle.at[:, :, :half_width].add(from_above)
    return middle.at[:, :, interior - half_width :].add(from_below)


def fold_columns(gradient, half_width):
    interior = gradient.shape[3] - 2 * half_width
    left_rim = gradient[:, :, :, :half_width]
    right_rim = gradient[:, :, :, interior + half_width :]
    middle = gradient[:, :, :, half_width : interior + half_width]
    from_right = passed_along(left_rim.astype(jnp.bfloat16), "col", -1).astype(left_rim.dtype)
    from_left = passed_along(right_rim.astype(jnp.bfloat16), "col", 1).astype(right_rim.dtype)
    middle = middle.at[:, :, :, :half_width].add(from_left)
    return middle.at[:, :, :, interior - half_width :].add(from_right)


def shards(object_field, probe_wave, positions, counts, amplitudes):
    probe_size = probe_wave.shape[1]
    half_width = probe_size // 2
    slot_total = positions.shape[2]
    tables = make_tables(probe_size)
    probe_field = (probe_wave[0], probe_wave[1])
    corners = positions.reshape(slot_total, 2)
    measured_all = amplitudes.reshape(slot_total, probe_size, probe_size)
    used_slots = counts.reshape(())
    current = object_field
    for iteration in range(ITERS):
        extended = padded(current.astype(jnp.bfloat16), (("row", 2), ("col", 3)), half_width)
        gradient = jnp.zeros(extended.shape, jnp.float32)

        def own_slot(slot_index, accumulated, weight):
            corner = lax.dynamic_index_in_dim(corners, slot_index, 0, keepdims=False)
            measured = lax.dynamic_index_in_dim(measured_all, slot_index, 0, keepdims=False)
            update = slot_gradient(
                window_at(extended, corner, probe_size), probe_field, measured, tables
            )
            return add_window(accumulated, corner, update * weight)

        def masked(slot_index, accumulated):
            weight = (slot_index < used_slots).astype(jnp.float32)
            return own_slot(slot_index, accumulated, weight)

        gradient = lax.fori_loop(0, slot_total, masked, gradient)
        summed = fold_columns(fold_rows(gradient, half_width), half_width)
        current = current - descent_rate * summed
    return current


def solution(mesh):
    in_specs = (
        P(None, None, "row", "col"),
        P(),
        P("row", "col", None, None),
        P("row", "col"),
        P("row", "col", None, None, None),
    )
    out_specs = P(None, None, "row", "col")
    return jax.shard_map(shards, mesh=mesh, in_specs=in_specs, out_specs=out_specs, check_vma=False)
```

profile of v0, /device:TPU:4, one launch (start us, length us, event | category | flops | bytes accessed | tf_op | source)
XLA Modules:
  0.0 587.8 jit_solution(12871860489257004638)
XLA Ops:
  3.5 7.3 %collective-permute-start.1 = (bf16[2,2,128,256]{2,3,1,0:T(8,128)(2,1)S(1)}, bf16[2,2,128,256]{2,3,1,0:T(8,128)(2,1)S(1)}, u32[]{:S(2)}, u32[]{:S(2)}) collective-permute-start(bf16[2,2,128,256]{2,3,1,0:T(8,128)(2,1)S(1)} %get-tuple-element.877), channel_id=1, source_target_pairs={{8,0},{16,8},{24,16},{32,24},{40,32},{48,40},{56,48},{64,56},{72,6... | collective-permute-start | bytes 786440 | tf_op jit(solution)/shard_map/ppermute | solution.py:29
  38.6 12.6 %collective-permute-done.3 = bf16[2,2,512,128]{2,3,1,0:T(8,128)(2,1)} collective-permute-done((bf16[2,2,512,128]{2,3,1,0:T(8,128)(2,1)S(1)}, bf16[2,2,512,128]{2,3,1,0:T(8,128)(2,1)}, u32[]{:S(2)}, u32[]{:S(2)}) %collective-permute-start.3) | collective-permute-done | bytes 524320 | tf_op jit(solution)/shard_map/ppermute | solution.py:29
  56.3 213.2 %while.38 = (s32[]{:T(128)}, f32[2,2,512,512]{3,2,1,0:T(8,128)}, s32[6,2]{0,1:T(2,128)S(1)}, bf16[6,256,256]{1,2,0:T(8,128)(2,1)}, bf16[2,2,512,512]{2,3,1,0:T(8...) while((s32[]{:T(128)}, f32[2,2,512,512]{3,2,1,0:T(8,128)}, ...), condition=%wide.region_1.2_spmd, body=%wide.region_0.1_spmd.sunk | while | flops 1084948480 | bytes 44958028 | solution.py:192
  79.9 12.3 %dynamic_update_slice.20 = f32[2,2,512,512]{3,2,1,0:T(8,128)} dynamic-update-slice(f32[2,2,512,512]{3,2,1,0:T(8,128)} %get-tuple-element.1227, f32[2,2,256,256]{3,2,1,0:T(8,128)S(1)} %copy.42, s32[]{:T(128)} %constant.328.clone.1..sunk, s32[]{:T(128)} %constant.328.clone.1..sunk, s32[]{:T(128)S(6)} %select_n.202, s32[]{:T(128)S(6)} %select_n.203) | dynamic-update-slice | bytes 2097156 | tf_op jit(solution)/shard_map/while/body/eval_jaxpr/dynamic_update_slice | solution.py:139
  115.8 11.2 %dynamic_update_slice.20 = f32[2,2,512,512]{3,2,1,0:T(8,128)} dynamic-update-slice(f32[2,2,512,512]{3,2,1,0:T(8,128)} %get-tuple-element.1227, f32[2,2,256,256]{3,2,1,0:T(8,128)S(1)} %copy.42, s32[]{:T(128)} %constant.328.clone.1..sunk, s32[]{:T(128)} %constant.328.clone.1..sunk, s32[]{:T(128)S(6)} %select_n.202, s32[]{:T(128)S(6)} %select_n.203) | dynamic-update-slice | bytes 2097156 | tf_op jit(solution)/shard_map/while/body/eval_jaxpr/dynamic_update_slice | solution.py:139
  150.7 11.5 %dynamic_update_slice.20 = f32[2,2,512,512]{3,2,1,0:T(8,128)} dynamic-update-slice(f32[2,2,512,512]{3,2,1,0:T(8,128)} %get-tuple-element.1227, f32[2,2,256,256]{3,2,1,0:T(8,128)S(1)} %copy.42, s32[]{:T(128)} %constant.328.clone.1..sunk, s32[]{:T(128)} %constant.328.clone.1..sunk, s32[]{:T(128)S(6)} %select_n.202, s32[]{:T(128)S(6)} %select_n.203) | dynamic-update-slice | bytes 2097156 | tf_op jit(solution)/shard_map/while/body/eval_jaxpr/dynamic_update_slice | solution.py:139
  185.9 12.2 %dynamic_update_slice.20 = f32[2,2,512,512]{3,2,1,0:T(8,128)} dynamic-update-slice(f32[2,2,512,512]{3,2,1,0:T(8,128)} %get-tuple-element.1227, f32[2,2,256,256]{3,2,1,0:T(8,128)S(1)} %copy.42, s32[]{:T(128)} %constant.328.clone.1..sunk, s32[]{:T(128)} %constant.328.clone.1..sunk, s32[]{:T(128)S(6)} %select_n.202, s32[]{:T(128)S(6)} %select_n.203) | dynamic-update-slice | bytes 2097156 | tf_op jit(solution)/shard_map/while/body/eval_jaxpr/dynamic_update_slice | solution.py:139
  221.8 12.1 %dynamic_update_slice.20 = f32[2,2,512,512]{3,2,1,0:T(8,128)} dynamic-update-slice(f32[2,2,512,512]{3,2,1,0:T(8,128)} %get-tuple-element.1227, f32[2,2,256,256]{3,2,1,0:T(8,128)S(1)} %copy.42, s32[]{:T(128)} %constant.328.clone.1..sunk, s32[]{:T(128)} %constant.328.clone.1..sunk, s32[]{:T(128)S(6)} %select_n.202, s32[]{:T(128)S(6)} %select_n.203) | dynamic-update-slice | bytes 2097156 | tf_op jit(solution)/shard_map/while/body/eval_jaxpr/dynamic_update_slice | solution.py:139
  257.5 11.9 %dynamic_update_slice.20 = f32[2,2,512,512]{3,2,1,0:T(8,128)} dynamic-update-slice(f32[2,2,512,512]{3,2,1,0:T(8,128)} %get-tuple-element.1227, f32[2,2,256,256]{3,2,1,0:T(8,128)S(1)} %copy.42, s32[]{:T(128)} %constant.328.clone.1..sunk, s32[]{:T(128)} %constant.328.clone.1..sunk, s32[]{:T(128)S(6)} %select_n.202, s32[]{:T(128)S(6)} %select_n.203) | dynamic-update-slice | bytes 2097156 | tf_op jit(solution)/shard_map/while/body/eval_jaxpr/dynamic_update_slice | solution.py:139
  274.1 7.3 %collective-permute-start.5 = (bf16[2,2,128,512]{3,2,1,0:T(8,128)(2,1)S(1)}, bf16[2,2,128,512]{3,2,1,0:T(8,128)(2,1)S(1)}, u32[]{:S(2)}, u32[]{:S(2)}) collective-permute-start(bf16[2,2,128,512]{3,2,1,0:T(8,128)(2,1)S(1)} %get-tuple-element.862), channel_id=1, source_target_pairs={{8,0},{16,8},{24,16},{32,24},{40,32},{48,40},{56,48},{64,56},{72,6... | collective-permute-start | bytes 1572872 | tf_op jit(solution)/shard_map/ppermute | solution.py:16
  281.5 4.8 collective-permute-done.4
  295.9 7.0 %collective-permute-done.7 = bf16[2,2,256,128]{3,2,1,0:T(8,128)(2,1)S(1)} collective-permute-done((bf16[2,2,256,128]{3,2,1,0:T(8,128)(2,1)S(1)}, bf16[2,2,256,128]{3,2,1,0:T(8,128)(2,1)S(1)}, u32[]{:S(2)}, u32[]{:S(2)}) %collective-permute-start.7) | collective-permute-done | bytes 262176 | tf_op jit(solution)/shard_map/ppermute | solution.py:16
  306.1 7.3 %collective-permute-start.9 = (bf16[2,2,128,256]{3,2,1,0:T(8,128)(2,1)S(1)}, bf16[2,2,128,256]{3,2,1,0:T(8,128)(2,1)S(1)}, u32[]{:S(2)}, u32[]{:S(2)}) collective-permute-start(bf16[2,2,128,256]{3,2,1,0:T(8,128)(2,1)S(1)} %get-tuple-element.873), channel_id=1, source_target_pairs={{8,0},{16,8},{24,16},{32,24},{40,32},{48,40},{56,48},{64,56},{72,6... | collective-permute-start | bytes 786440 | tf_op jit(solution)/shard_map/ppermute | solution.py:29
  328.1 15.6 %collective-permute-done.11 = bf16[2,2,512,128]{3,2,1,0:T(8,128)(2,1)} collective-permute-done((bf16[2,2,512,128]{3,2,1,0:T(8,128)(2,1)S(1)}, bf16[2,2,512,128]{3,2,1,0:T(8,128)(2,1)}, u32[]{:S(2)}, u32[]{:S(2)}) %collective-permute-start.11) | collective-permute-done | bytes 524320 | tf_op jit(solution)/shard_map/ppermute | solution.py:29
  347.6 208.5 %while.39 = (s32[]{:T(128)}, f32[2,2,512,512]{3,2,1,0:T(8,128)}, s32[6,2]{0,1:T(2,128)S(1)}, bf16[6,256,256]{1,2,0:T(8,128)(2,1)}, bf16[2,2,512,512]{3,2,1,0:T(8...) while((s32[]{:T(128)}, f32[2,2,512,512]{3,2,1,0:T(8,128)}, ...), condition=%wide.region_3.4_spmd, body=%wide.region_2.3_spmd.sunk | while | flops 1084948480 | bytes 63832452 | solution.py:192
  370.3 12.4 %dynamic_update_slice.21 = f32[2,2,512,512]{3,2,1,0:T(8,128)} dynamic-update-slice(f32[2,2,512,512]{3,2,1,0:T(8,128)} %get-tuple-element.1287, f32[2,2,256,256]{3,2,1,0:T(8,128)S(1)} %copy.45, s32[]{:T(128)} %constant.328.clone.1..sunk.1, s32[]{:T(128)} %constant.328.clone.1..sunk.1, s32[]{:T(128)S(6)} %select_n.204, s32[]{:T(128)S(6)} %select_n.205) | dynamic-update-slice | bytes 2097156 | tf_op jit(solution)/shard_map/while/body/eval_jaxpr/dynamic_update_slice | solution.py:139
  405.5 11.4 %dynamic_update_slice.21 = f32[2,2,512,512]{3,2,1,0:T(8,128)} dynamic-update-slice(f32[2,2,512,512]{3,2,1,0:T(8,128)} %get-tuple-element.1287, f32[2,2,256,256]{3,2,1,0:T(8,128)S(1)} %copy.45, s32[]{:T(128)} %constant.328.clone.1..sunk.1, s32[]{:T(128)} %constant.328.clone.1..sunk.1, s32[]{:T(128)S(6)} %select_n.204, s32[]{:T(128)S(6)} %select_n.205) | dynamic-update-slice | bytes 2097156 | tf_op jit(solution)/shard_map/while/body/eval_jaxpr/dynamic_update_slice | solution.py:139
  439.6 11.6 %dynamic_update_slice.21 = f32[2,2,512,512]{3,2,1,0:T(8,128)} dynamic-update-slice(f32[2,2,512,512]{3,2,1,0:T(8,128)} %get-tuple-element.1287, f32[2,2,256,256]{3,2,1,0:T(8,128)S(1)} %copy.45, s32[]{:T(128)} %constant.328.clone.1..sunk.1, s32[]{:T(128)} %constant.328.clone.1..sunk.1, s32[]{:T(128)S(6)} %select_n.204, s32[]{:T(128)S(6)} %select_n.205) | dynamic-update-slice | bytes 2097156 | tf_op jit(solution)/shard_map/while/body/eval_jaxpr/dynamic_update_slice | solution.py:139
  473.9 12.4 %dynamic_update_slice.21 = f32[2,2,512,512]{3,2,1,0:T(8,128)} dynamic-update-slice(f32[2,2,512,512]{3,2,1,0:T(8,128)} %get-tuple-element.1287, f32[2,2,256,256]{3,2,1,0:T(8,128)S(1)} %copy.45, s32[]{:T(128)} %constant.328.clone.1..sunk.1, s32[]{:T(128)} %constant.328.clone.1..sunk.1, s32[]{:T(128)S(6)} %select_n.204, s32[]{:T(128)S(6)} %select_n.205) | dynamic-update-slice | bytes 2097156 | tf_op jit(solution)/shard_map/while/body/eval_jaxpr/dynamic_update_slice | solution.py:139
  509.0 12.2 %dynamic_update_slice.21 = f32[2,2,512,512]{3,2,1,0:T(8,128)} dynamic-update-slice(f32[2,2,512,512]{3,2,1,0:T(8,128)} %get-tuple-element.1287, f32[2,2,256,256]{3,2,1,0:T(8,128)S(1)} %copy.45, s32[]{:T(128)} %constant.328.clone.1..sunk.1, s32[]{:T(128)} %constant.328.clone.1..sunk.1, s32[]{:T(128)S(6)} %select_n.204, s32[]{:T(128)S(6)} %select_n.205) | dynamic-update-slice | bytes 2097156 | tf_op jit(solution)/shard_map/while/body/eval_jaxpr/dynamic_update_slice | solution.py:139
  544.0 12.1 %dynamic_update_slice.21 = f32[2,2,512,512]{3,2,1,0:T(8,128)} dynamic-update-slice(f32[2,2,512,512]{3,2,1,0:T(8,128)} %get-tuple-element.1287, f32[2,2,256,256]{3,2,1,0:T(8,128)S(1)} %copy.45, s32[]{:T(128)} %constant.328.clone.1..sunk.1, s32[]{:T(128)} %constant.328.clone.1..sunk.1, s32[]{:T(128)S(6)} %select_n.204, s32[]{:T(128)S(6)} %select_n.205) | dynamic-update-slice | bytes 2097156 | tf_op jit(solution)/shard_map/while/body/eval_jaxpr/dynamic_update_slice | solution.py:139
  560.7 7.3 %collective-permute-start.13 = (bf16[2,2,128,512]{3,2,1,0:T(8,128)(2,1)S(1)}, bf16[2,2,128,512]{3,2,1,0:T(8,128)(2,1)S(1)}, u32[]{:S(2)}, u32[]{:S(2)}) collective-permute-start(bf16[2,2,128,512]{3,2,1,0:T(8,128)(2,1)S(1)} %get-tuple-element.860), channel_id=1, source_target_pairs={{8,0},{16,8},{24,16},{32,24},{40,32},{48,40},{56,48},{64,56},{72,6... | collective-permute-start | bytes 1572872 | tf_op jit(solution)/shard_map/ppermute | solution.py:16
  568.2 4.8 collective-permute-done.12
  580.4 6.0 %collective-permute-done.15 = bf16[2,2,256,128]{3,2,1,0:T(8,128)(2,1)S(1)} collective-permute-done((bf16[2,2,256,128]{3,2,1,0:T(8,128)(2,1)S(1)}, bf16[2,2,256,128]{3,2,1,0:T(8,128)(2,1)S(1)}, u32[]{:S(2)}, u32[]{:S(2)}) %collective-permute-start.15) | collective-permute-done | bytes 262176 | tf_op jit(solution)/shard_map/ppermute | solution.py:16
  (453 shorter events, 306.7 us)
Async XLA Ops:
  1.5 23.7 %collective-permute-start = (bf16[2,2,128,256]{2,3,1,0:T(8,128)(2,1)S(1)}, bf16[2,2,128,256]{2,3,1,0:T(8,128)(2,1)S(1)}, u32[]{:S(2)}, u32[]{:S(2)}) collective-permute-start(bf16[2,2,128,256]{2,3,1,0:T(8,128)(2,1)S(1)} %get-tuple-element.876), channel_id=1, source_target_pairs={{0,8},{8,16},{16,24},{24,32},{32,40},{40,48},{48,56},{56,64},{64,7... | collective-permute-start | bytes 786440 | tf_op jit(solution)/shard_map/ppermute | solution.py:27
  3.5 21.8 %collective-permute-start.1 = (bf16[2,2,128,256]{2,3,1,0:T(8,128)(2,1)S(1)}, bf16[2,2,128,256]{2,3,1,0:T(8,128)(2,1)S(1)}, u32[]{:S(2)}, u32[]{:S(2)}) collective-permute-start(bf16[2,2,128,256]{2,3,1,0:T(8,128)(2,1)S(1)} %get-tuple-element.877), channel_id=1, source_target_pairs={{8,0},{16,8},{24,16},{32,24},{40,32},{48,40},{56,48},{64,56},{72,6... | collective-permute-start | bytes 786440 | tf_op jit(solution)/shard_map/ppermute | solution.py:29
  26.3 12.3 %collective-permute-start.2 = (bf16[2,2,512,128]{2,3,1,0:T(8,128)(2,1)}, bf16[2,2,512,128]{2,3,1,0:T(8,128)(2,1)}, u32[]{:S(2)}, u32[]{:S(2)}) collective-permute-start(bf16[2,2,512,128]{2,3,1,0:T(8,128)(2,1)} %get-tuple-element.870), channel_id=1, source_target_pairs={{0,1},{1,2},{2,3},{3,4},{4,5},{5,6},{6,7},{8,9},{9,10},{10,11},{11... | collective-permute-start | bytes 1572872 | tf_op jit(solution)/shard_map/ppermute | solution.py:27
  31.0 20.3 %collective-permute-start.3 = (bf16[2,2,512,128]{2,3,1,0:T(8,128)(2,1)S(1)}, bf16[2,2,512,128]{2,3,1,0:T(8,128)(2,1)}, u32[]{:S(2)}, u32[]{:S(2)}) collective-permute-start(bf16[2,2,512,128]{2,3,1,0:T(8,128)(2,1)S(1)} %get-tuple-element.871), channel_id=1, source_target_pairs={{1,0},{2,1},{3,2},{4,3},{5,4},{6,5},{7,6},{9,8},{10,9},{11,10},{12... | collective-permute-start | bytes 1572872 | tf_op jit(solution)/shard_map/ppermute | solution.py:29
  269.5 11.9 %copy-start.1 = (f32[2,2,512,512]{3,2,1,0:T(8,128)S(1)}, f32[2,2,512,512]{3,2,1,0:T(8,128)}, u32[]{:S(2)}) copy-start(f32[2,2,512,512]{3,2,1,0:T(8,128)} %get-tuple-element.719) | copy-start | bytes 12582916
  272.2 14.2 %collective-permute-start.4 = (bf16[2,2,128,512]{3,2,1,0:T(8,128)(2,1)S(1)}, bf16[2,2,128,512]{3,2,1,0:T(8,128)(2,1)S(1)}, u32[]{:S(2)}, u32[]{:S(2)}) collective-permute-start(bf16[2,2,128,512]{3,2,1,0:T(8,128)(2,1)S(1)} %get-tuple-element.863), channel_id=1, source_target_pairs={{0,8},{8,16},{16,24},{24,32},{32,40},{40,48},{48,56},{56,64},{64,7... | collective-permute-start | bytes 1572872 | tf_op jit(solution)/shard_map/ppermute | solution.py:16
  274.1 14.0 %collective-permute-start.5 = (bf16[2,2,128,512]{3,2,1,0:T(8,128)(2,1)S(1)}, bf16[2,2,128,512]{3,2,1,0:T(8,128)(2,1)S(1)}, u32[]{:S(2)}, u32[]{:S(2)}) collective-permute-start(bf16[2,2,128,512]{3,2,1,0:T(8,128)(2,1)S(1)} %get-tuple-element.862), channel_id=1, source_target_pairs={{8,0},{16,8},{24,16},{32,24},{40,32},{48,40},{56,48},{64,56},{72,6... | collective-permute-start | bytes 1572872 | tf_op jit(solution)/shard_map/ppermute | solution.py:16
  288.6 7.2 %collective-permute-start.6 = (bf16[2,2,256,128]{3,2,1,0:T(8,128)(2,1)S(1)}, bf16[2,2,256,128]{3,2,1,0:T(8,128)(2,1)S(1)}, u32[]{:S(2)}, u32[]{:S(2)}) collective-permute-start(bf16[2,2,256,128]{3,2,1,0:T(8,128)(2,1)S(1)} %get-tuple-element.869), channel_id=1, source_target_pairs={{0,1},{1,2},{2,3},{3,4},{4,5},{5,6},{6,7},{8,9},{9,10},{10,11},{11... | collective-permute-start | bytes 786440 | tf_op jit(solution)/shard_map/ppermute | solution.py:16
  289.9 14.0 %copy-start.6 = (f32[2,2,256,256]{3,2,1,0:T(8,128)S(1)}, f32[2,2,256,256]{3,2,1,0:T(8,128)}, u32[]{:S(2)}) copy-start(f32[2,2,256,256]{3,2,1,0:T(8,128)} %param.25) | copy-start | bytes 3145732
  289.9 12.9 %collective-permute-start.7 = (bf16[2,2,256,128]{3,2,1,0:T(8,128)(2,1)S(1)}, bf16[2,2,256,128]{3,2,1,0:T(8,128)(2,1)S(1)}, u32[]{:S(2)}, u32[]{:S(2)}) collective-permute-start(bf16[2,2,256,128]{3,2,1,0:T(8,128)(2,1)S(1)} %get-tuple-element.868), channel_id=1, source_target_pairs={{1,0},{2,1},{3,2},{4,3},{5,4},{6,5},{7,6},{9,8},{10,9},{11,10},{12... | collective-permute-start | bytes 786440 | tf_op jit(solution)/shard_map/ppermute | solution.py:16
  304.2 11.4 %collective-permute-start.8 = (bf16[2,2,128,256]{3,2,1,0:T(8,128)(2,1)S(1)}, bf16[2,2,128,256]{3,2,1,0:T(8,128)(2,1)S(1)}, u32[]{:S(2)}, u32[]{:S(2)}) collective-permute-start(bf16[2,2,128,256]{3,2,1,0:T(8,128)(2,1)S(1)} %get-tuple-element.872), channel_id=1, source_target_pairs={{0,8},{8,16},{16,24},{24,32},{32,40},{40,48},{48,56},{56,64},{64,7... | collective-permute-start | bytes 786440 | tf_op jit(solution)/shard_map/ppermute | solution.py:27
  306.1 11.2 %collective-permute-start.9 = (bf16[2,2,128,256]{3,2,1,0:T(8,128)(2,1)S(1)}, bf16[2,2,128,256]{3,2,1,0:T(8,128)(2,1)S(1)}, u32[]{:S(2)}, u32[]{:S(2)}) collective-permute-start(bf16[2,2,128,256]{3,2,1,0:T(8,128)(2,1)S(1)} %get-tuple-element.873), channel_id=1, source_target_pairs={{8,0},{16,8},{24,16},{32,24},{40,32},{48,40},{56,48},{64,56},{72,6... | collective-permute-start | bytes 786440 | tf_op jit(solution)/shard_map/ppermute | solution.py:29
  317.6 10.6 %collective-permute-start.10 = (bf16[2,2,512,128]{3,2,1,0:T(8,128)(2,1)S(1)}, bf16[2,2,512,128]{3,2,1,0:T(8,128)(2,1)}, u32[]{:S(2)}, u32[]{:S(2)}) collective-permute-start(bf16[2,2,512,128]{3,2,1,0:T(8,128)(2,1)S(1)} %get-tuple-element.866), channel_id=1, source_target_pairs={{0,1},{1,2},{2,3},{3,4},{4,5},{5,6},{6,7},{8,9},{9,10},{10,11},{11... | collective-permute-start | bytes 1572872 | tf_op jit(solution)/shard_map/ppermute | solution.py:27
  322.2 21.5 %collective-permute-start.11 = (bf16[2,2,512,128]{3,2,1,0:T(8,128)(2,1)S(1)}, bf16[2,2,512,128]{3,2,1,0:T(8,128)(2,1)}, u32[]{:S(2)}, u32[]{:S(2)}) collective-permute-start(bf16[2,2,512,128]{3,2,1,0:T(8,128)(2,1)S(1)} %get-tuple-element.867), channel_id=1, source_target_pairs={{1,0},{2,1},{3,2},{4,3},{5,4},{6,5},{7,6},{9,8},{10,9},{11,10},{12... | collective-permute-start | bytes 1572872 | tf_op jit(solution)/shard_map/ppermute | solution.py:29
  370.3 12.4 %copy-start.5 = (bf16[2,2,512,512]{3,2,1,0:T(8,128)(2,1)S(1)}, bf16[2,2,512,512]{3,2,1,0:T(8,128)(2,1)}, u32[]{:S(2)}) copy-start(bf16[2,2,512,512]{3,2,1,0:T(8,128)(2,1)} %copy-done.4) | copy-start | bytes 6291460 | tf_op jit(solution)/shard_map/while
  439.6 11.6 %copy-start.5 = (bf16[2,2,512,512]{3,2,1,0:T(8,128)(2,1)S(1)}, bf16[2,2,512,512]{3,2,1,0:T(8,128)(2,1)}, u32[]{:S(2)}) copy-start(bf16[2,2,512,512]{3,2,1,0:T(8,128)(2,1)} %copy-done.4) | copy-start | bytes 6291460 | tf_op jit(solution)/shard_map/while
  473.9 12.4 %copy-start.5 = (bf16[2,2,512,512]{3,2,1,0:T(8,128)(2,1)S(1)}, bf16[2,2,512,512]{3,2,1,0:T(8,128)(2,1)}, u32[]{:S(2)}) copy-start(bf16[2,2,512,512]{3,2,1,0:T(8,128)(2,1)} %copy-done.4) | copy-start | bytes 6291460 | tf_op jit(solution)/shard_map/while
  509.0 12.2 %copy-start.5 = (bf16[2,2,512,512]{3,2,1,0:T(8,128)(2,1)S(1)}, bf16[2,2,512,512]{3,2,1,0:T(8,128)(2,1)}, u32[]{:S(2)}) copy-start(bf16[2,2,512,512]{3,2,1,0:T(8,128)(2,1)} %copy-done.4) | copy-start | bytes 6291460 | tf_op jit(solution)/shard_map/while
  544.0 12.1 %copy-start.5 = (bf16[2,2,512,512]{3,2,1,0:T(8,128)(2,1)S(1)}, bf16[2,2,512,512]{3,2,1,0:T(8,128)(2,1)}, u32[]{:S(2)}) copy-start(bf16[2,2,512,512]{3,2,1,0:T(8,128)(2,1)} %copy-done.4) | copy-start | bytes 6291460 | tf_op jit(solution)/shard_map/while
  556.1 11.9 %copy-start = (f32[2,2,512,512]{3,2,1,0:T(8,128)S(1)}, f32[2,2,512,512]{3,2,1,0:T(8,128)}, u32[]{:S(2)}) copy-start(f32[2,2,512,512]{3,2,1,0:T(8,128)} %get-tuple-element.720) | copy-start | bytes 12582916
  558.8 14.2 %collective-permute-start.12 = (bf16[2,2,128,512]{3,2,1,0:T(8,128)(2,1)S(1)}, bf16[2,2,128,512]{3,2,1,0:T(8,128)(2,1)S(1)}, u32[]{:S(2)}, u32[]{:S(2)}) collective-permute-start(bf16[2,2,128,512]{3,2,1,0:T(8,128)(2,1)S(1)} %get-tuple-element.861), channel_id=1, source_target_pairs={{0,8},{8,16},{16,24},{24,32},{32,40},{40,48},{48,56},{56,64},{64,7... | collective-permute-start | bytes 1572872 | tf_op jit(solution)/shard_map/ppermute | solution.py:16
  560.7 13.9 %collective-permute-start.13 = (bf16[2,2,128,512]{3,2,1,0:T(8,128)(2,1)S(1)}, bf16[2,2,128,512]{3,2,1,0:T(8,128)(2,1)S(1)}, u32[]{:S(2)}, u32[]{:S(2)}) collective-permute-start(bf16[2,2,128,512]{3,2,1,0:T(8,128)(2,1)S(1)} %get-tuple-element.860), channel_id=1, source_target_pairs={{8,0},{16,8},{24,16},{32,24},{40,32},{48,40},{56,48},{64,56},{72,6... | collective-permute-start | bytes 1572872 | tf_op jit(solution)/shard_map/ppermute | solution.py:16
  575.2 5.2 collective-permute-start.14
  576.5 10.0 %collective-permute-start.15 = (bf16[2,2,256,128]{3,2,1,0:T(8,128)(2,1)S(1)}, bf16[2,2,256,128]{3,2,1,0:T(8,128)(2,1)S(1)}, u32[]{:S(2)}, u32[]{:S(2)}) collective-permute-start(bf16[2,2,256,128]{3,2,1,0:T(8,128)(2,1)S(1)} %get-tuple-element.864), channel_id=1, source_target_pairs={{1,0},{2,1},{3,2},{4,3},{5,4},{6,5},{7,6},{9,8},{10,9},{11,10},{12... | collective-permute-start | bytes 786440 | tf_op jit(solution)/shard_map/ppermute | solution.py:16
  (13 other events, 87.6 us)
where the time goes:
time: 598 us; the launch traced here: 588 us
  local copies, waits for them, and re-layouts  196 us (33%)
  matrix products  135 us (23%)
  other arithmetic  76.5 us (13%)
  waiting for transfers between devices  69.1 us (12%)
  loops' own time  57.3 us (10%)
  starting transfers between devices  54.1 us (9%)
    dynamic_update_slice x24, local copies, waits for them, and re-layouts, add_window(): lax.dynamic_update_slice(accumulated, current + update, (anchor, anchor,...  147 us
    dot_general x48, matrix products, apply_right(): result = jnp.dot(stacked, joined, preferred_element_type=jnp.float32)  62 us
    dot_general x48, matrix products, apply_left(): result = jnp.dot(stacked, joined, preferred_element_type=jnp.float32)  61.4 us
    another operation x2, loops' own time, shards(): gradient = lax.fori_loop(0, slot_total, masked, gradient)  57.3 us
    ppermute x8, waiting for transfers between devices, passed_along(): lax.ppermute(value, axis, [(source, source + steps) for source in range(l...  32.3 us
    convert_element_type x108, other arithmetic, to_half(): return (operand[0].astype(jnp.bfloat16), operand[1].astype(jnp.bfloat16))  30.9 us
    ppermute x4, waiting for transfers between devices, padded(): lax.ppermute(head, axis, [((i + 1) % count, i) for i in range(ends)])  30 us
    dynamic_slice x36, local copies, waits for them, and re-layouts, window_at(): lax.dynamic_slice(source, (anchor, anchor, corner[0], corner[1]), (2, 2,...  28.7 us
  transfers between devices with their start and end apart: 16, of which 13 were waited for; matrix products, arithmetic and copies ran while one was open for 4% of the time, Pallas kernels for 0%

commit v1 on v0

v1 whole, which is shorter than its diff:
```python
import functools
import jax, jax.numpy as jnp
from jax import lax
import numpy as np
from jax.experimental import pallas as pl
from jax.experimental.pallas import tpu as pltpu
from jax.sharding import PartitionSpec as P

ITERS = 2
RATE = 0.1

N = 256
F32, BF16 = jnp.float32, jnp.bfloat16


def tables():
    k = np.arange(N)
    ang = 2 * np.pi * ((k[:, None] * k[None, :]) % N) / N
    f = np.exp(-1j * ang) / 16.0
    fk = np.where(k < N // 2, k, k - N).astype(np.float64)
    ker = (np.exp(-1j * np.pi * fk * fk / (2 * N))[None, :] * np.exp(1j * ang)).sum(1) / N
    p = ker[(k[:, None] - k[None, :]) % N]

    def block(m):
        return np.block([[m.real, -m.imag], [m.imag, m.real]]).astype(jnp.bfloat16)

    return np.stack([block(f), block(f.conj()), block(p), block(p.conj())])


def dot(a, b):
    return jnp.dot(a, b, preferred_element_type=F32)


def body(j, y, x, refs, LM, RM, RC):
    ext, grad, xs, yh, mid, sec, probe, amps, tab = refs
    q = x // 128
    s = x - q * 128
    back = (128 - s) % 128

    def lanes(rows):
        return lax.broadcasted_iota(jnp.int32, (rows, 128), 1)

    def window(p, r0, rows):
        parts = [pltpu.roll(ext[p, q + t, pl.ds(y + r0, rows), :], back, 1) for t in range(3)]
        keep = lanes(rows) < 128 - s
        return [jnp.where(keep, parts[t], parts[t + 1]) for t in range(2)]

    def cut(i, _):
        r0 = pl.multiple_of(i * RC, RC)
        wr, wi = window(0, r0, RC), window(1, r0, RC)
        sr, si = window(2, r0, RC), window(3, r0, RC)
        for t in range(2):
            cols = pl.ds(128 * t, 128)
            pr, pi = probe[0, pl.ds(r0, RC), cols], probe[1, pl.ds(r0, RC), cols]
            fr, fi = 1.0 + wr[t], wi[t]
            xs[pl.ds(r0, RC), cols] = (pr * fr - pi * fi).astype(BF16)
            xs[pl.ds(N + r0, RC), cols] = (pr * fi + pi * fr).astype(BF16)
            sec[0, pl.ds(r0, RC), cols] = 1.0 + sr[t]
            sec[1, pl.ds(r0, RC), cols] = si[t]
        return 0

    lax.fori_loop(0, N // RC, cut, 0, unroll=True)

    def left(m):
        for a in range(0, 2 * N, LM):
            out = dot(tab[m, a:a + LM, :], xs[...]).astype(BF16)
            if LM == 2 * N:
                yh[:, :N] = out[:N]
                yh[:, N:] = out[N:]
            else:
                yh[a % N:a % N + LM, (a // N) * N:(a // N) * N + N] = out

    def right(m, use):
        for a in range(0, N, RM):
            z = dot(yh[a:a + RM, :], tab[m, :, :])
            use(slice(a, a + RM), z[:, :N], z[:, N:])

    def put(rs, zr, zi):
        mr, mi = zr.astype(BF16), zi.astype(BF16)
        mid[0, rs, :] = mr
        mid[1, rs, :] = mi
        mr, mi = mr.astype(F32), mi.astype(F32)
        sr, si = sec[0, rs, :], sec[1, rs, :]
        xs[rs, :] = (mr * sr - mi * si).astype(BF16)
        xs[N + rs.start:N + rs.stop, :] = (mr * si + mi * sr).astype(BF16)

    left(2)
    right(3, put)

    def resid(rs, zr, zi):
        a = amps[j, rs, :].astype(F32)
        f = 1.0 - a * lax.rsqrt(zr * zr + zi * zi + 0.25)
        xs[rs, :] = (f * zr).astype(BF16)
        xs[N + rs.start:N + rs.stop, :] = (f * zi).astype(BF16)

    left(0)
    right(1, resid)

    def accumulate(p, rs, g):
        rows = rs.stop - rs.start
        g0, g1 = pltpu.roll(g[:, :128], s, 1), pltpu.roll(g[:, 128:], s, 1)
        hi = lanes(rows) >= s
        zero = jnp.zeros((rows, 128), F32)
        at = pl.ds(y + rs.start, rows)
        grad[p, q, at, :] += jnp.where(hi, g0, zero)
        grad[p, q + 1, at, :] += jnp.where(hi, g1, g0)
        grad[p, q + 2, at, :] += jnp.where(hi, zero, g1)

    def far(rs, zr, zi):
        mr, mi = mid[0, rs, :].astype(F32), mid[1, rs, :].astype(F32)
        accumulate(2, rs, zr * mr + zi * mi)
        accumulate(3, rs, zi * mr - zr * mi)
        sr, si = sec[0, rs, :], sec[1, rs, :]
        xs[rs, :] = (zr * sr + zi * si).astype(BF16)
        xs[N + rs.start:N + rs.stop, :] = (zi * sr - zr * si).astype(BF16)

    left(1)
    right(0, far)

    def near(rs, zr, zi):
        pr, pi = probe[0, rs, :], probe[1, rs, :]
        accumulate(0, rs, zr * pr + zi * pi)
        accumulate(1, rs, zi * pr - zr * pi)

    left(3)
    right(2, near)


def kernel(LM, RM, RC, cnt, pos, obj, hl, hr, hu, hd, probe, amps, tab, up, down, mids, ext, grad, xs, yh, mid, sec):
    for p in range(4):
        a, b = divmod(p, 2)
        for t in range(4):
            cols = slice(128 * t, 128 * t + 128)
            ext[p, t, 0:128, :] = hu[a, b, :, cols].astype(F32)
            ext[p, t, 384:512, :] = hd[a, b, :, cols].astype(F32)
        ext[p, 0, 128:384, :] = hl[a, b].astype(F32)
        ext[p, 3, 128:384, :] = hr[a, b].astype(F32)
        ext[p, 1, 128:384, :] = obj[a, b, :, 0:128].astype(BF16).astype(F32)
        ext[p, 2, 128:384, :] = obj[a, b, :, 128:256].astype(BF16).astype(F32)
    grad[...] = jnp.zeros(grad.shape, F32)
    refs = (ext, grad, xs, yh, mid, sec, probe, amps, tab)

    def step(j, _):
        body(j, pos[j, 0], pos[j, 1], refs, LM, RM, RC)
        return 0

    lax.fori_loop(0, cnt[0], step, 0)
    for p in range(4):
        a, b = divmod(p, 2)
        for t in range(4):
            cols = slice(128 * t, 128 * t + 128)
            up[a, b, :, cols] = grad[p, t, 0:128, :].astype(BF16)
            down[a, b, :, cols] = grad[p, t, 384:512, :].astype(BF16)
            mids[a, b, :, cols] = grad[p, t, 128:384, :]


def slots(cnt, pos, obj, hl, hr, hu, hd, probe, amps, tab, LM=256, RM=128, RC=32):
    V = pl.BlockSpec(memory_space=pltpu.VMEM)
    S = pl.BlockSpec(memory_space=pltpu.SMEM)
    return pl.pallas_call(
        functools.partial(kernel, LM, RM, RC),
        out_shape=(jax.ShapeDtypeStruct((2, 2, 128, 512), BF16), jax.ShapeDtypeStruct((2, 2, 128, 512), BF16),
                   jax.ShapeDtypeStruct((2, 2, 256, 512), F32)),
        in_specs=[S, S] + [V] * 8,
        out_specs=[V] * 3,
        scratch_shapes=[pltpu.VMEM((4, 5, 512, 128), F32), pltpu.VMEM((4, 5, 512, 128), F32),
                        pltpu.VMEM((512, 256), BF16), pltpu.VMEM((256, 512), BF16),
                        pltpu.VMEM((2, 256, 256), BF16), pltpu.VMEM((2, 256, 256), F32)],
        compiler_params=pltpu.CompilerParams(vmem_limit_bytes=48 << 20),
    )(cnt, pos, obj, hl, hr, hu, hd, probe, amps, tab)


def passed(value, axis, steps):
    count = lax.axis_size(axis)
    first, last = max(0, -steps), min(count, count - steps)
    return lax.ppermute(value, axis, [(i, i + steps) for i in range(first, last)])


def row_halos(band):
    return passed(band[:, :, 128:], "row", 1), passed(band[:, :, :128], "row", -1)


def shards(obj, probe, positions, counts, amplitudes):
    pos = positions.reshape(6, 2)
    cnt = counts.reshape(1)
    amps = amplitudes.reshape(6, N, N)
    tab = jnp.asarray(tables())
    column = lax.axis_index("col")
    half = obj.astype(BF16)
    hl = passed(half[..., 128:], "col", 1)
    hr = passed(half[..., :128], "col", -1)
    for it in range(ITERS):
        hu, hd = row_halos(jnp.concatenate([hl, obj.astype(BF16), hr], 3))
        up, down, mids = slots(cnt, pos, obj, hl, hr, hu, hd, probe, amps, tab)
        above, below = passed(down, "row", 1), passed(up, "row", -1)
        total = mids + jnp.concatenate([above, below], 2).astype(F32)
        if it + 1 < ITERS:
            right = passed(total[..., :256].astype(BF16), "col", -1).astype(F32)
            left = passed(total[..., 256:].astype(BF16), "col", 1).astype(F32)
            total = total + jnp.concatenate([left, right], 3)
            hl = jnp.where(column > 0, hl.astype(F32) - RATE * total[..., :128], 0.0).astype(BF16)
            hr = jnp.where(column + 1 < lax.axis_size("col"), hr.astype(F32) - RATE * total[..., 384:], 0.0).astype(BF16)
            obj = obj - RATE * total[..., 128:384]
        else:
            right = passed(total[..., :128].astype(BF16), "col", -1).astype(F32)
            left = passed(total[..., 384:].astype(BF16), "col", 1).astype(F32)
            obj = obj - RATE * (total[..., 128:384] + jnp.concatenate([left, right], 3))
    return obj


def solution(mesh):
    return jax.shard_map(
        shards,
        mesh=mesh,
        in_specs=(P(None, None, "row", "col"), P(), P("row", "col", None, None), P("row", "col"),
                  P("row", "col", None, None, None)),
        out_specs=P(None, None, "row", "col"),
        check_vma=False,
    )
```

time: 598 us -> 166 us (0.28)
  the two profiles are of different devices: /device:TPU:4 before, /device:TPU:20 now
where the time goes in v1:
time: 166 us; the launch traced here: 167 us
  waiting for transfers between devices  72.5 us (44%)
  starting transfers between devices  63.5 us (38%)
  Pallas kernels  17.9 us (11%)
  other arithmetic  9.84 us (6%)
  local copies, waits for them, and re-layouts  2.46 us (1%)
    ppermute x14, waiting for transfers between devices, passed(): lax.ppermute(value, axis, [(i, i + steps) for i in range(first, last)])  72.5 us
    ppermute x14, starting transfers between devices, passed(): lax.ppermute(value, axis, [(i, i + steps) for i in range(first, last)])  63.5 us
    pallas_call x2, Pallas kernels, slots(): pl.pallas_call(functools.partial(kernel, LM, RM, RC), out_shape=(jax.Shap...  17.9 us
    another operation x2, other arithmetic  4.23 us
  transfers between devices with their start and end apart: 14, of which 14 were waited for; matrix products, arithmetic and copies ran while one was open for 0% of the time, Pallas kernels for 0%

profile of v1, /device:TPU:20, one launch (start us, length us, event | category | flops | bytes accessed | tf_op | source)
XLA Modules:
  0.0 167.1 jit_solution(15437767569843512593)
XLA Ops:
  1.4 3.0 %collective-permute-start.1 = (bf16[2,2,256,128]{3,2,1,0:T(8,128)(2,1)S(1)}, bf16[2,2,256,128]{3,2,1,0:T(8,128)(2,1)S(1)}, u32[]{:S(2)}, u32[]{:S(2)}) collective-permute-start(bf16[2,2,256,128]{3,2,1,0:T(8,128)(2,1)S(1)} %get-tuple-element.31), channel_id=1, source_target_pairs={{1,0},{2,1},{3,2},{4,3},{5,4},{6,5},{7,6},{9,8},{10,9},{11,10},{12... | collective-permute-start | bytes 786440 | tf_op jit(solution)/shard_map/ppermute | solution.py:176
  4.4 3.0 %collective-permute-start = (bf16[2,2,256,128]{3,2,1,0:T(8,128)(2,1)S(1)}, bf16[2,2,256,128]{3,2,1,0:T(8,128)(2,1)S(1)}, u32[]{:S(2)}, u32[]{:S(2)}) collective-permute-start(bf16[2,2,256,128]{3,2,1,0:T(8,128)(2,1)S(1)} %get-tuple-element.32), channel_id=1, source_target_pairs={{0,1},{1,2},{2,3},{3,4},{4,5},{5,6},{6,7},{8,9},{9,10},{10,11},{11... | collective-permute-start | bytes 786440 | tf_op jit(solution)/shard_map/ppermute | solution.py:176
  7.4 5.0 %collective-permute-done.1.hr = bf16[2,2,256,128]{3,2,1,0:T(8,128)(2,1)S(1)} collective-permute-done((bf16[2,2,256,128]{3,2,1,0:T(8,128)(2,1)S(1)}, bf16[2,2,256,128]{3,2,1,0:T(8,128)(2,1)S(1)}, u32[]{:S(2)}, u32[]{:S(2)}) %collective-permute-start.1) | collective-permute-done | bytes 262176 | tf_op jit(solution)/shard_map/ppermute | solution.py:176
  12.5 4.4 %collective-permute-done.hl = bf16[2,2,256,128]{3,2,1,0:T(8,128)(2,1)S(1)} collective-permute-done((bf16[2,2,256,128]{3,2,1,0:T(8,128)(2,1)S(1)}, bf16[2,2,256,128]{3,2,1,0:T(8,128)(2,1)S(1)}, u32[]{:S(2)}, u32[]{:S(2)}) %collective-permute-start) | collective-permute-done | bytes 262176 | tf_op jit(solution)/shard_map/ppermute | solution.py:176
  18.0 6.3 %collective-permute-start.3 = (bf16[2,2,128,512]{3,2,1,0:T(8,128)(2,1)}, bf16[2,2,128,512]{3,2,1,0:T(8,128)(2,1)S(1)}, u32[]{:S(2)}, u32[]{:S(2)}) collective-permute-start(bf16[2,2,128,512]{3,2,1,0:T(8,128)(2,1)} %get-tuple-element.29), channel_id=1, source_target_pairs={{8,0},{16,8},{24,16},{32,24},{40,32},{48,40},{56,48},{64,56},{72,6... | collective-permute-start | bytes 1572872 | tf_op jit(solution)/shard_map/ppermute | solution.py:176
  27.0 4.3 %collective-permute-done.3.hd = bf16[2,2,128,512]{3,2,1,0:T(8,128)(2,1)S(1)} collective-permute-done((bf16[2,2,128,512]{3,2,1,0:T(8,128)(2,1)}, bf16[2,2,128,512]{3,2,1,0:T(8,128)(2,1)S(1)}, u32[]{:S(2)}, u32[]{:S(2)}) %collective-permute-start.3) | collective-permute-done | bytes 524320 | tf_op jit(solution)/shard_map/ppermute | solution.py:176
  31.3 7.4 %collective-permute-done.2.hu = bf16[2,2,128,512]{3,2,1,0:T(8,128)(2,1)} collective-permute-done((bf16[2,2,128,512]{3,2,1,0:T(8,128)(2,1)}, bf16[2,2,128,512]{3,2,1,0:T(8,128)(2,1)}, u32[]{:S(2)}, u32[]{:S(2)}) %collective-permute-start.2) | collective-permute-done | bytes 524320 | tf_op jit(solution)/shard_map/ppermute | solution.py:176
  38.7 9.1 %shard_map.64 = (bf16[2,2,128,512]{3,2,1,0:T(8,128)(2,1)S(1)}, bf16[2,2,128,512]{3,2,1,0:T(8,128)(2,1)S(1)}, f32[2,2,256,512]{3,2,1,0:T(8,128)}) custom-call(s32[1]{0:T(128)} %bitcast.3.cnt, s32[6,2]{1,0:T(8,128)S(1)} %copy.7.pos, f32[2,2,256,256]{3,2,1,0:T(8,128)S(1)} %copy-done, bf16[2,2,256,128]{3,2,1,0:T(8,128)(2,1)S(1)} %collective-permute-done.hl, ...), custom_call_target="tpu_custom_call" | custom-call | tf_op jit(solution)/shard_map/pallas_call | solution.py:160
  49.7 11.3 %collective-permute-start.5 = (bf16[2,2,128,512]{3,2,1,0:T(8,128)(2,1)S(1)}, bf16[2,2,128,512]{3,2,1,0:T(8,128)(2,1)S(1)}, u32[]{:S(2)}, u32[]{:S(2)}) collective-permute-start(bf16[2,2,128,512]{3,2,1,0:T(8,128)(2,1)S(1)} %get-tuple-element.13), channel_id=1, source_target_pairs={{8,0},{16,8},{24,16},{32,24},{40,32},{48,40},{56,48},{64,56},{72,6... | collective-permute-start | bytes 1572872 | tf_op jit(solution)/shard_map/ppermute | solution.py:176
  61.0 5.0 %collective-permute-done.4 = bf16[2,2,128,512]{3,2,1,0:T(8,128)(2,1)S(1)} collective-permute-done((bf16[2,2,128,512]{3,2,1,0:T(8,128)(2,1)S(1)}, bf16[2,2,128,512]{3,2,1,0:T(8,128)(2,1)S(1)}, u32[]{:S(2)}, u32[]{:S(2)}) %collective-permute-start.4) | collective-permute-done | bytes 524320 | tf_op jit(solution)/shard_map/ppermute | solution.py:176
  67.7 2.2 %fusion = bf16[2,2,256,512]{3,2,1,0:T(8,128)(2,1)S(1)} fusion(f32[2,2,256,512]{3,2,1,0:T(8,128)} %get-tuple-element.11, bf16[2,2,128,512]{3,2,1,0:T(8,128)(2,1)S(1)} %collective-permute-done.5, bf16[2,2,128,512]{3,2,1,0:T(8,128)(2,1)S(1)} %collective-permute-done.4), kind=kLoop, calls=%fused_computation.3 | loop fusion | flops 3145728 | bytes 4194304 | tf_op jit(solution)/shard_map/convert.5
  72.9 4.8 %collective-permute-start.7 = (bf16[2,2,256,256]{3,2,1,0:T(8,128)(2,1)}, bf16[2,2,256,256]{3,2,1,0:T(8,128)(2,1)}, u32[]{:S(2)}, u32[]{:S(2)}) collective-permute-start(bf16[2,2,256,256]{3,2,1,0:T(8,128)(2,1)} %get-tuple-element.28), channel_id=1, source_target_pairs={{1,0},{2,1},{3,2},{4,3},{5,4},{6,5},{7,6},{9,8},{10,9},{11,10},{12... | collective-permute-start | bytes 1572872 | tf_op jit(solution)/shard_map/ppermute | solution.py:176
  77.7 11.1 %collective-permute-done.6 = bf16[2,2,256,256]{3,2,1,0:T(8,128)(2,1)} collective-permute-done((bf16[2,2,256,256]{3,2,1,0:T(8,128)(2,1)}, bf16[2,2,256,256]{3,2,1,0:T(8,128)(2,1)}, u32[]{:S(2)}, u32[]{:S(2)}) %collective-permute-start.6) | collective-permute-done | bytes 524320 | tf_op jit(solution)/shard_map/ppermute | solution.py:176
  88.8 6.4 %collective-permute-done.7 = bf16[2,2,256,256]{3,2,1,0:T(8,128)(2,1)} collective-permute-done((bf16[2,2,256,256]{3,2,1,0:T(8,128)(2,1)}, bf16[2,2,256,256]{3,2,1,0:T(8,128)(2,1)}, u32[]{:S(2)}, u32[]{:S(2)}) %collective-permute-start.7) | collective-permute-done | bytes 524320 | tf_op jit(solution)/shard_map/ppermute | solution.py:176
  95.3 2.4 %convert_add_fusion.1 = f32[2,2,256,512]{3,2,1,0:T(8,128)S(1)} fusion(f32[2,2,256,512]{3,2,1,0:T(8,128)} %get-tuple-element.11, bf16[2,2,256,256]{3,2,1,0:T(8,128)(2,1)} %collective-permute-done.7, bf16[2,2,256,256]{3,2,1,0:T(8,128)(2,1)} %collective-permute-done.6, bf16[2,2,128,512]{3,2,1,0:T(8,128)(2,1)} %copy-done.3, ...), kind=kLoop, calls=%fused_computation.1 | loop fusion | flops 5242880 | bytes 6291456 | tf_op jit(solution)/shard_map/add | solution.py:200
  98.4 7.4 %collective-permute-start.9 = (bf16[2,2,128,512]{3,2,1,0:T(8,128)(2,1)S(1)}, bf16[2,2,128,512]{3,2,1,0:T(8,128)(2,1)S(1)}, u32[]{:S(2)}, u32[]{:S(2)}) collective-permute-start(bf16[2,2,128,512]{3,2,1,0:T(8,128)(2,1)S(1)} %get-tuple-element.25), channel_id=1, source_target_pairs={{8,0},{16,8},{24,16},{32,24},{40,32},{48,40},{56,48},{64,56},{72,6... | collective-permute-start | bytes 1572872 | tf_op jit(solution)/shard_map/ppermute | solution.py:176
  107.7 4.7 %collective-permute-done.9.hd = bf16[2,2,128,512]{3,2,1,0:T(8,128)(2,1)S(1)} collective-permute-done((bf16[2,2,128,512]{3,2,1,0:T(8,128)(2,1)S(1)}, bf16[2,2,128,512]{3,2,1,0:T(8,128)(2,1)S(1)}, u32[]{:S(2)}, u32[]{:S(2)}) %collective-permute-start.9) | collective-permute-done | bytes 524320 | tf_op jit(solution)/shard_map/ppermute | solution.py:176
  112.5 7.4 %collective-permute-done.8.hu = bf16[2,2,128,512]{3,2,1,0:T(8,128)(2,1)S(1)} collective-permute-done((bf16[2,2,128,512]{3,2,1,0:T(8,128)(2,1)S(1)}, bf16[2,2,128,512]{3,2,1,0:T(8,128)(2,1)S(1)}, u32[]{:S(2)}, u32[]{:S(2)}) %collective-permute-start.8) | collective-permute-done | bytes 524320 | tf_op jit(solution)/shard_map/ppermute | solution.py:176
  119.9 8.9 %shard_map.65 = (bf16[2,2,128,512]{3,2,1,0:T(8,128)(2,1)S(1)}, bf16[2,2,128,512]{3,2,1,0:T(8,128)(2,1)S(1)}, f32[2,2,256,512]{3,2,1,0:T(8,128)}) custom-call(s32[1]{0:T(128)} %bitcast.4.cnt, s32[6,2]{1,0:T(8,128)S(1)} %copy.7.pos, f32[2,2,256,256]{3,2,1,0:T(8,128)S(1)} %get-tuple-element.20.obj, bf16[2,2,256,128]{3,2,1,0:T(8,128)(2,1)S(1)} %get-tuple-element.22.hl, ...), custom_call_target="tpu_custom_call" | custom-call | tf_op jit(solution)/shard_map/pallas_call | solution.py:160
  130.7 11.4 %collective-permute-start.11 = (bf16[2,2,128,512]{3,2,1,0:T(8,128)(2,1)S(1)}, bf16[2,2,128,512]{3,2,1,0:T(8,128)(2,1)S(1)}, u32[]{:S(2)}, u32[]{:S(2)}) collective-permute-start(bf16[2,2,128,512]{3,2,1,0:T(8,128)(2,1)S(1)} %get-tuple-element.16), channel_id=1, source_target_pairs={{8,0},{16,8},{24,16},{32,24},{40,32},{48,40},{56,48},{64,56},{72,6... | collective-permute-start | bytes 1572872 | tf_op jit(solution)/shard_map/ppermute | solution.py:176
  142.1 5.0 %collective-permute-done.10 = bf16[2,2,128,512]{3,2,1,0:T(8,128)(2,1)S(1)} collective-permute-done((bf16[2,2,128,512]{3,2,1,0:T(8,128)(2,1)S(1)}, bf16[2,2,128,512]{3,2,1,0:T(8,128)(2,1)S(1)}, u32[]{:S(2)}, u32[]{:S(2)}) %collective-permute-start.10) | collective-permute-done | bytes 524320 | tf_op jit(solution)/shard_map/ppermute | solution.py:176
  152.9 4.8 %collective-permute-start.13 = (bf16[2,2,256,128]{3,2,1,0:T(8,128)(2,1)S(1)}, bf16[2,2,256,128]{3,2,1,0:T(8,128)(2,1)S(1)}, u32[]{:S(2)}, u32[]{:S(2)}) collective-permute-start(bf16[2,2,256,128]{3,2,1,0:T(8,128)(2,1)S(1)} %get-tuple-element.24), channel_id=1, source_target_pairs={{1,0},{2,1},{3,2},{4,3},{5,4},{6,5},{7,6},{9,8},{10,9},{11,10},{12... | collective-permute-start | bytes 786440 | tf_op jit(solution)/shard_map/ppermute | solution.py:176
  157.7 2.4 %collective-permute-done.12 = bf16[2,2,256,128]{3,2,1,0:T(8,128)(2,1)S(1)} collective-permute-done((bf16[2,2,256,128]{3,2,1,0:T(8,128)(2,1)S(1)}, bf16[2,2,256,128]{3,2,1,0:T(8,128)(2,1)S(1)}, u32[]{:S(2)}, u32[]{:S(2)}) %collective-permute-start.12) | collective-permute-done | bytes 262176 | tf_op jit(solution)/shard_map/ppermute | solution.py:176
  160.1 5.7 %collective-permute-done.13 = bf16[2,2,256,128]{3,2,1,0:T(8,128)(2,1)S(1)} collective-permute-done((bf16[2,2,256,128]{3,2,1,0:T(8,128)(2,1)S(1)}, bf16[2,2,256,128]{3,2,1,0:T(8,128)(2,1)S(1)}, u32[]{:S(2)}, u32[]{:S(2)}) %collective-permute-start.13) | collective-permute-done | bytes 262176 | tf_op jit(solution)/shard_map/ppermute | solution.py:176
  (31 shorter events, 22.6 us)
Async XLA Ops:
  1.4 11.1 %collective-permute-start.1 = (bf16[2,2,256,128]{3,2,1,0:T(8,128)(2,1)S(1)}, bf16[2,2,256,128]{3,2,1,0:T(8,128)(2,1)S(1)}, u32[]{:S(2)}, u32[]{:S(2)}) collective-permute-start(bf16[2,2,256,128]{3,2,1,0:T(8,128)(2,1)S(1)} %get-tuple-element.31), channel_id=1, source_target_pairs={{1,0},{2,1},{3,2},{4,3},{5,4},{6,5},{7,6},{9,8},{10,9},{11,10},{12... | collective-permute-start | bytes 786440 | tf_op jit(solution)/shard_map/ppermute | solution.py:176
  4.4 22.5 %copy-start.4 = (s32[1,1,6,2]{2,3,1,0:T(2,128)S(1)}, s32[1,1,6,2]{2,3,1,0:T(2,128)}, u32[]{:S(2)}) copy-start(s32[1,1,6,2]{2,3,1,0:T(2,128)} %param.8) | copy-start | bytes 148
  4.4 34.3 %copy-start = (f32[2,2,256,256]{3,2,1,0:T(8,128)S(1)}, f32[2,2,256,256]{3,2,1,0:T(8,128)}, u32[]{:S(2)}) copy-start(f32[2,2,256,256]{3,2,1,0:T(8,128)} %obj.1) | copy-start | bytes 3145732
  4.4 34.3 %copy-start.1 = (bf16[1,1,6,256,256]{4,3,2,1,0:T(8,128)(2,1)S(1)}, bf16[1,1,6,256,256]{4,3,2,1,0:T(8,128)(2,1)}, u32[]{:S(2)}) copy-start(bf16[1,1,6,256,256]{4,3,2,1,0:T(8,128)(2,1)} %param.10) | copy-start | bytes 2359300
  4.4 34.3 %copy-start.2 = (f32[2,256,256]{2,1,0:T(8,128)S(1)}, f32[2,256,256]{2,1,0:T(8,128)}, u32[]{:S(2)}) copy-start(f32[2,256,256]{2,1,0:T(8,128)} %probe.3) | copy-start | bytes 1572868
  4.4 12.4 %collective-permute-start = (bf16[2,2,256,128]{3,2,1,0:T(8,128)(2,1)S(1)}, bf16[2,2,256,128]{3,2,1,0:T(8,128)(2,1)S(1)}, u32[]{:S(2)}, u32[]{:S(2)}) collective-permute-start(bf16[2,2,256,128]{3,2,1,0:T(8,128)(2,1)S(1)} %get-tuple-element.32), channel_id=1, source_target_pairs={{0,1},{1,2},{2,3},{3,4},{4,5},{5,6},{6,7},{8,9},{9,10},{10,11},{11... | collective-permute-start | bytes 786440 | tf_op jit(solution)/shard_map/ppermute | solution.py:176
  18.0 13.3 %collective-permute-start.3 = (bf16[2,2,128,512]{3,2,1,0:T(8,128)(2,1)}, bf16[2,2,128,512]{3,2,1,0:T(8,128)(2,1)S(1)}, u32[]{:S(2)}, u32[]{:S(2)}) collective-permute-start(bf16[2,2,128,512]{3,2,1,0:T(8,128)(2,1)} %get-tuple-element.29), channel_id=1, source_target_pairs={{8,0},{16,8},{24,16},{32,24},{40,32},{48,40},{56,48},{64,56},{72,6... | collective-permute-start | bytes 1572872 | tf_op jit(solution)/shard_map/ppermute | solution.py:176
  24.3 14.4 %collective-permute-start.2 = (bf16[2,2,128,512]{3,2,1,0:T(8,128)(2,1)}, bf16[2,2,128,512]{3,2,1,0:T(8,128)(2,1)}, u32[]{:S(2)}, u32[]{:S(2)}) collective-permute-start(bf16[2,2,128,512]{3,2,1,0:T(8,128)(2,1)} %get-tuple-element.30), channel_id=1, source_target_pairs={{0,8},{8,16},{16,24},{24,32},{32,40},{40,48},{48,56},{56,64},{64,7... | collective-permute-start | bytes 1572872 | tf_op jit(solution)/shard_map/ppermute | solution.py:176
  47.8 18.2 %collective-permute-start.4 = (bf16[2,2,128,512]{3,2,1,0:T(8,128)(2,1)S(1)}, bf16[2,2,128,512]{3,2,1,0:T(8,128)(2,1)S(1)}, u32[]{:S(2)}, u32[]{:S(2)}) collective-permute-start(bf16[2,2,128,512]{3,2,1,0:T(8,128)(2,1)S(1)} %get-tuple-element.12), channel_id=1, source_target_pairs={{0,8},{8,16},{16,24},{24,32},{32,40},{40,48},{48,56},{56,64},{64,7... | collective-permute-start | bytes 1572872 | tf_op jit(solution)/shard_map/ppermute | solution.py:176
  49.7 18.0 %collective-permute-start.5 = (bf16[2,2,128,512]{3,2,1,0:T(8,128)(2,1)S(1)}, bf16[2,2,128,512]{3,2,1,0:T(8,128)(2,1)S(1)}, u32[]{:S(2)}, u32[]{:S(2)}) collective-permute-start(bf16[2,2,128,512]{3,2,1,0:T(8,128)(2,1)S(1)} %get-tuple-element.13), channel_id=1, source_target_pairs={{8,0},{16,8},{24,16},{32,24},{40,32},{48,40},{56,48},{64,56},{72,6... | collective-permute-start | bytes 1572872 | tf_op jit(solution)/shard_map/ppermute | solution.py:176
  67.7 2.2 %copy-start.3 = (bf16[2,2,128,512]{3,2,1,0:T(8,128)(2,1)}, bf16[2,2,128,512]{3,2,1,0:T(8,128)(2,1)S(1)}, u32[]{:S(2)}) copy-start(bf16[2,2,128,512]{3,2,1,0:T(8,128)(2,1)S(1)} %collective-permute-done.5) | copy-start | bytes 1572868
  70.9 17.9 %collective-permute-start.6 = (bf16[2,2,256,256]{3,2,1,0:T(8,128)(2,1)}, bf16[2,2,256,256]{3,2,1,0:T(8,128)(2,1)}, u32[]{:S(2)}, u32[]{:S(2)}) collective-permute-start(bf16[2,2,256,256]{3,2,1,0:T(8,128)(2,1)} %get-tuple-element.27), channel_id=1, source_target_pairs={{0,1},{1,2},{2,3},{3,4},{4,5},{5,6},{6,7},{8,9},{9,10},{10,11},{11... | collective-permute-start | bytes 1572872 | tf_op jit(solution)/shard_map/ppermute | solution.py:176
  72.9 22.4 %collective-permute-start.7 = (bf16[2,2,256,256]{3,2,1,0:T(8,128)(2,1)}, bf16[2,2,256,256]{3,2,1,0:T(8,128)(2,1)}, u32[]{:S(2)}, u32[]{:S(2)}) collective-permute-start(bf16[2,2,256,256]{3,2,1,0:T(8,128)(2,1)} %get-tuple-element.28), channel_id=1, source_target_pairs={{1,0},{2,1},{3,2},{4,3},{5,4},{6,5},{7,6},{9,8},{10,9},{11,10},{12... | collective-permute-start | bytes 1572872 | tf_op jit(solution)/shard_map/ppermute | solution.py:176
  98.4 14.1 %collective-permute-start.9 = (bf16[2,2,128,512]{3,2,1,0:T(8,128)(2,1)S(1)}, bf16[2,2,128,512]{3,2,1,0:T(8,128)(2,1)S(1)}, u32[]{:S(2)}, u32[]{:S(2)}) collective-permute-start(bf16[2,2,128,512]{3,2,1,0:T(8,128)(2,1)S(1)} %get-tuple-element.25), channel_id=1, source_target_pairs={{8,0},{16,8},{24,16},{32,24},{40,32},{48,40},{56,48},{64,56},{72,6... | collective-permute-start | bytes 1572872 | tf_op jit(solution)/shard_map/ppermute | solution.py:176
  105.8 14.1 %collective-permute-start.8 = (bf16[2,2,128,512]{3,2,1,0:T(8,128)(2,1)S(1)}, bf16[2,2,128,512]{3,2,1,0:T(8,128)(2,1)S(1)}, u32[]{:S(2)}, u32[]{:S(2)}) collective-permute-start(bf16[2,2,128,512]{3,2,1,0:T(8,128)(2,1)S(1)} %get-tuple-element.26), channel_id=1, source_target_pairs={{0,8},{8,16},{16,24},{24,32},{32,40},{40,48},{48,56},{56,64},{64,7... | collective-permute-start | bytes 1572872 | tf_op jit(solution)/shard_map/ppermute | solution.py:176
  128.8 18.3 %collective-permute-start.10 = (bf16[2,2,128,512]{3,2,1,0:T(8,128)(2,1)S(1)}, bf16[2,2,128,512]{3,2,1,0:T(8,128)(2,1)S(1)}, u32[]{:S(2)}, u32[]{:S(2)}) collective-permute-start(bf16[2,2,128,512]{3,2,1,0:T(8,128)(2,1)S(1)} %get-tuple-element.15), channel_id=1, source_target_pairs={{0,8},{8,16},{16,24},{24,32},{32,40},{40,48},{48,56},{56,64},{64,7... | collective-permute-start | bytes 1572872 | tf_op jit(solution)/shard_map/ppermute | solution.py:176
  130.7 18.1 %collective-permute-start.11 = (bf16[2,2,128,512]{3,2,1,0:T(8,128)(2,1)S(1)}, bf16[2,2,128,512]{3,2,1,0:T(8,128)(2,1)S(1)}, u32[]{:S(2)}, u32[]{:S(2)}) collective-permute-start(bf16[2,2,128,512]{3,2,1,0:T(8,128)(2,1)S(1)} %get-tuple-element.16), channel_id=1, source_target_pairs={{8,0},{16,8},{24,16},{32,24},{40,32},{48,40},{56,48},{64,56},{72,6... | collective-permute-start | bytes 1572872 | tf_op jit(solution)/shard_map/ppermute | solution.py:176
  150.9 9.2 %collective-permute-start.12 = (bf16[2,2,256,128]{3,2,1,0:T(8,128)(2,1)S(1)}, bf16[2,2,256,128]{3,2,1,0:T(8,128)(2,1)S(1)}, u32[]{:S(2)}, u32[]{:S(2)}) collective-permute-start(bf16[2,2,256,128]{3,2,1,0:T(8,128)(2,1)S(1)} %get-tuple-element.23), channel_id=1, source_target_pairs={{0,1},{1,2},{2,3},{3,4},{4,5},{5,6},{6,7},{8,9},{9,10},{10,11},{11... | collective-permute-start | bytes 786440 | tf_op jit(solution)/shard_map/ppermute | solution.py:176
  152.9 13.0 %collective-permute-start.13 = (bf16[2,2,256,128]{3,2,1,0:T(8,128)(2,1)S(1)}, bf16[2,2,256,128]{3,2,1,0:T(8,128)(2,1)S(1)}, u32[]{:S(2)}, u32[]{:S(2)}) collective-permute-start(bf16[2,2,256,128]{3,2,1,0:T(8,128)(2,1)S(1)} %get-tuple-element.24), channel_id=1, source_target_pairs={{1,0},{2,1},{3,2},{4,3},{5,4},{6,5},{7,6},{9,8},{10,9},{11,10},{12... | collective-permute-start | bytes 786440 | tf_op jit(solution)/shard_map/ppermute | solution.py:176

commit v2 on v1

v2 whole, which is shorter than its diff:
```python
import functools
import jax, jax.numpy as jnp
from jax import lax
import numpy as np
from jax.experimental import pallas as pl
from jax.experimental.pallas import tpu as pltpu
from jax.sharding import PartitionSpec as P

RATE = 0.1
H = 128

N = 256
F32, BF16 = jnp.float32, jnp.bfloat16


def tables():
    k = np.arange(N)
    ang = 2 * np.pi * ((k[:, None] * k[None, :]) % N) / N
    f = np.exp(-1j * ang) / 16.0
    fk = np.where(k < N // 2, k, k - N).astype(np.float64)
    ker = (np.exp(-1j * np.pi * fk * fk / (2 * N))[None, :] * np.exp(1j * ang)).sum(1) / N
    p = ker[(k[:, None] - k[None, :]) % N]

    return np.stack([f.real, f.imag, p.real, p.imag]).astype(jnp.bfloat16)


def dot(a, b):
    return jnp.dot(a, b, preferred_element_type=F32)


def body(j, y, x, refs, LM, RM, RC):
    ext, grad, xs, yh, mid, sec, probe, amps, tab = refs
    q = x // 128
    s = x - q * 128
    back = (128 - s) % 128

    def lanes(rows):
        return lax.broadcasted_iota(jnp.int32, (rows, 128), 1)

    def window(p, r0, rows):
        parts = [pltpu.roll(ext[p, q + t, pl.ds(y + r0, rows), :], back, 1) for t in range(3)]
        keep = lanes(rows) < 128 - s
        return [jnp.where(keep, parts[t], parts[t + 1]) for t in range(2)]

    def cut(i, _):
        r0 = pl.multiple_of(i * RC, RC)
        wr, wi = window(0, r0, RC), window(1, r0, RC)
        sr, si = window(2, r0, RC), window(3, r0, RC)
        for t in range(2):
            cols = pl.ds(128 * t, 128)
            pr, pi = probe[0, pl.ds(r0, RC), cols], probe[1, pl.ds(r0, RC), cols]
            fr, fi = 1.0 + wr[t], wi[t]
            xs[pl.ds(r0, RC), cols] = (pr * fr - pi * fi).astype(BF16)
            xs[pl.ds(N + r0, RC), cols] = (pr * fi + pi * fr).astype(BF16)
            sec[0, pl.ds(r0, RC), cols] = 1.0 + sr[t]
            sec[1, pl.ds(r0, RC), cols] = si[t]
        return 0

    lax.fori_loop(0, N // RC, cut, 0, unroll=True)

    def left(m):
        for a in range(0, 2 * N, LM):
            out = dot(tab[m, a:a + LM, :], xs[...]).astype(BF16)
            if LM == 2 * N:
                yh[:, :N] = out[:N]
                yh[:, N:] = out[N:]
            else:
                yh[a % N:a % N + LM, (a // N) * N:(a // N) * N + N] = out

    def right(m, use):
        for a in range(0, N, RM):
            z = dot(yh[a:a + RM, :], tab[m, :, :])
            use(slice(a, a + RM), z[:, :N], z[:, N:])

    def put(rs, zr, zi):
        mr, mi = zr.astype(BF16), zi.astype(BF16)
        mid[0, rs, :] = mr
        mid[1, rs, :] = mi
        mr, mi = mr.astype(F32), mi.astype(F32)
        sr, si = sec[0, rs, :], sec[1, rs, :]
        xs[rs, :] = (mr * sr - mi * si).astype(BF16)
        xs[N + rs.start:N + rs.stop, :] = (mr * si + mi * sr).astype(BF16)

    left(2)
    right(3, put)

    def resid(rs, zr, zi):
        a = amps[j, rs, :].astype(F32)
        f = 1.0 - a * lax.rsqrt(zr * zr + zi * zi + 0.25)
        xs[rs, :] = (f * zr).astype(BF16)
        xs[N + rs.start:N + rs.stop, :] = (f * zi).astype(BF16)

    left(0)
    right(1, resid)

    def accumulate(p, rs, g):
        rows = rs.stop - rs.start
        g0, g1 = pltpu.roll(g[:, :128], s, 1), pltpu.roll(g[:, 128:], s, 1)
        hi = lanes(rows) >= s
        zero = jnp.zeros((rows, 128), F32)
        at = pl.ds(y + rs.start, rows)
        grad[p, q, at, :] += jnp.where(hi, g0, zero)
        grad[p, q + 1, at, :] += jnp.where(hi, g1, g0)
        grad[p, q + 2, at, :] += jnp.where(hi, zero, g1)

    def far(rs, zr, zi):
        mr, mi = mid[0, rs, :].astype(F32), mid[1, rs, :].astype(F32)
        accumulate(2, rs, zr * mr + zi * mi)
        accumulate(3, rs, zi * mr - zr * mi)
        sr, si = sec[0, rs, :], sec[1, rs, :]
        xs[rs, :] = (zr * sr + zi * si).astype(BF16)
        xs[N + rs.start:N + rs.stop, :] = (zi * sr - zr * si).astype(BF16)

    left(1)
    right(0, far)

    def near(rs, zr, zi):
        pr, pi = probe[0, rs, :], probe[1, rs, :]
        accumulate(0, rs, zr * pr + zi * pi)
        accumulate(1, rs, zi * pr - zr * pi)

    left(3)
    right(2, near)


PLANES = [(a, b) for a in range(2) for b in range(2)]
VM = pl.BlockSpec(memory_space=pltpu.VMEM)
SM = pl.BlockSpec(memory_space=pltpu.SMEM)


def local(fn, outs, specs, scratch=(), flops=0, moved=1 << 20, vmem=12 << 20):
    return pl.pallas_call(
        fn,
        out_shape=tuple(jax.ShapeDtypeStruct(s, d) for s, d in outs),
        in_specs=specs,
        out_specs=tuple(VM for _ in outs),
        scratch_shapes=list(scratch),
        cost_estimate=pl.CostEstimate(flops=flops, bytes_accessed=moved, transcendentals=0),
        compiler_params=pltpu.CompilerParams(vmem_limit_bytes=vmem),
    )


def parity():
    return lax.rem(lax.axis_index("row"), 2)


def block(k):
    return pl.multiple_of(jnp.where(parity() == 0, H * k, H * (3 - k)), H)


def own(k):
    return pl.multiple_of(jnp.where(parity() == k, 0, H), H)


def slots_kernel(LM, RM, RC, cnt, pos, ez, ec, hz, hc, probe, amps, tab, rz, rc, mz, mc,
                 ext, grad, xs, yh, mid, sec):
    for k, strip in enumerate((hz, ez, ec, hc)):
        at = pl.ds(block(k), H)
        for p, (a, b) in enumerate(PLANES):
            for t in range(4):
                ext[p, t, at, :] = strip[a, b, :, H * t:H * t + H].astype(F32)
    grad[...] = jnp.zeros(grad.shape, F32)
    refs = (ext, grad, xs, yh, mid, sec, probe, amps, tab)

    def step(j, _):
        body(j, pos[j, 0], pos[j, 1], refs, LM, RM, RC)
        return 0

    lax.fori_loop(0, cnt[0], step, 0)
    for k, strip in enumerate((rz, mz, mc, rc)):
        at = pl.ds(block(k), H)
        for p, (a, b) in enumerate(PLANES):
            for t in range(4):
                strip[a, b, :, H * t:H * t + H] = grad[p, t, at, :].astype(strip.dtype)


def slots(cnt, pos, ez, ec, hz, hc, probe, amps, tab, LM=256, RM=128, RC=32):
    s = (2, 2, H, 512)
    return local(
        functools.partial(slots_kernel, LM, RM, RC),
        [(s, BF16), (s, BF16), (s, F32), (s, F32)],
        [SM, SM] + [VM] * 7,
        [pltpu.VMEM((4, 5, 512, H), F32), pltpu.VMEM((4, 5, 512, H), F32),
         pltpu.VMEM((512, N), BF16), pltpu.VMEM((N, 512), BF16),
         pltpu.VMEM((2, N, N), BF16), pltpu.VMEM((2, N, N), F32)],
        flops=1 << 33, vmem=30 << 20,
    )(cnt, pos, ez, ec, hz, hc, probe, amps, tab)


def matrices_kernel(base, tab):
    for m in range(2):
        re, im = base[2 * m], base[2 * m + 1]
        for conj in range(2):
            k = 2 * m + conj
            tab[k, 0:N, 0:N] = re
            tab[k, N:, N:] = re
            tab[k, 0:N, N:] = im if conj else -im
            tab[k, N:, 0:N] = -im if conj else im


def edges_kernel(obj, lz, rz, lc, rc):
    for k, (left, right) in enumerate(((lz, rz), (lc, rc))):
        at = pl.ds(own(k), H)
        for a, b in PLANES:
            left[a, b] = obj[a, b, at, 0:H].astype(BF16)
            right[a, b] = obj[a, b, at, N - H:N].astype(BF16)


def join_kernel(k, obj, hl, hr, e):
    at = pl.ds(own(k), H)
    for a, b in PLANES:
        e[a, b, :, 0:H] = hl[a, b]
        e[a, b, :, H:3 * H] = obj[a, b, at, :].astype(BF16)
        e[a, b, :, 3 * H:] = hr[a, b]


def bands_kernel(width, m, rim, *outs):
    r0 = 0
    for i in range(0, len(outs), 2):
        rows = outs[i].shape[2]
        rs = slice(r0, r0 + rows)
        for a, b in PLANES:
            outs[i][a, b] = (m[a, b, rs, 0:width] + rim[a, b, rs, 0:width].astype(F32)).astype(BF16)
            outs[i + 1][a, b] = (m[a, b, rs, 512 - width:] + rim[a, b, rs, 512 - width:].astype(F32)).astype(BF16)
        r0 += rows


def update_kernel(k, chunks, m, rim, obj, e, *rest):
    arrived, (e_new, o_new) = rest[:2 * chunks], rest[2 * chunks:]
    column = lax.axis_index("col")
    keep_left = (column > 0).astype(F32)
    keep_right = (column < lax.axis_size("col") - 1).astype(F32)
    r0 = 0
    for i in range(chunks):
        from_left, from_right = arrived[2 * i], arrived[2 * i + 1]
        rows = from_left.shape[2]
        rs = slice(r0, r0 + rows)
        at = pl.ds(own(k) + r0, rows)
        for a, b in PLANES:
            for side, other, keep, c0 in ((0, from_left, keep_left, 0), (1, from_right, keep_right, N)):
                cols = slice(c0, c0 + N)
                total = RATE * (m[a, b, rs, cols] + rim[a, b, rs, cols].astype(F32) + other[a, b].astype(F32))
                outer = slice(0, H) if side == 0 else slice(H, N)
                inner = slice(H, N) if side == 0 else slice(0, H)
                halo = slice(0, H) if side == 0 else slice(3 * H, 4 * H)
                mine = slice(0, H) if side == 0 else slice(H, N)
                old = e[a, b, rs, halo].astype(F32)
                e_new[a, b, rs, halo] = (keep * (old - total[:, outer])).astype(BF16)
                value = obj[a, b, at, mine] - total[:, inner]
                o_new[a, b, rs, mine] = value
                e_new[a, b, rs, slice(H + mine.start, H + mine.stop)] = value.astype(BF16)
        r0 += rows


def finish_kernel(mz, rimz, oz, lz, rz, mc, rimc, oc, lc, rc, out):
    for k, (m, rim, o, left, right) in enumerate(((mz, rimz, oz, lz, rz), (mc, rimc, oc, lc, rc))):
        at = pl.ds(own(k), H)
        for a, b in PLANES:
            for side, other in ((0, left), (1, right)):
                cols = slice(H + H * side, 2 * H + H * side)
                mine = slice(H * side, H * side + H)
                total = m[a, b, :, cols] + rim[a, b, :, cols].astype(F32) + other[a, b].astype(F32)
                out[a, b, at, mine] = o[a, b, :, mine] - RATE * total


def moved(value, axis, steps):
    count = lax.axis_size(axis)
    first, last = max(0, -steps), min(count, count - steps)
    return lax.ppermute(value, axis, [(i, i + steps) for i in range(first, last)])


def swapped(value, first):
    count = lax.axis_size("row")
    pairs = [(i, i + 1) for i in range(first, count - 1, 2)]
    return lax.ppermute(value, "row", pairs + [(j, i) for i, j in pairs])


def sideways(left, right):
    return moved(right, "col", 1), moved(left, "col", -1)


def program(obj, probe, positions, counts, amplitudes):
    pos = positions.reshape(6, 2)
    cnt = counts.reshape(1)
    amps = amplitudes.reshape(6, N, N)
    strip, cut, band = (2, 2, H, 512), (2, 2, H, H), (2, 2, H, N)
    part = (2, 2, H // 2, N)

    lz, rz, lc, rc = local(edges_kernel, [(cut, BF16)] * 4, [VM])(obj)
    hl, hr = sideways(lz, rz)
    gl, gr = sideways(lc, rc)
    (ez,) = local(functools.partial(join_kernel, 0), [(strip, BF16)], [VM] * 3)(obj, hl, hr)
    hz = swapped(ez, 1)
    (ec,) = local(functools.partial(join_kernel, 1), [(strip, BF16)], [VM] * 3)(obj, gl, gr)
    hc = swapped(ec, 0)
    (tab,) = local(matrices_kernel, [((4, 2 * N, 2 * N), BF16)], [VM])(jnp.asarray(tables()))
    rim_z, rim_c, mz, mc = slots(cnt, pos, ez, ec, hz, hc, probe, amps, tab)

    in_c = swapped(rim_c, 0)
    in_z = swapped(rim_z, 1)
    l1, r1, l2, r2 = local(functools.partial(bands_kernel, N), [(part, BF16)] * 4, [VM] * 2)(mc, in_c)
    a1 = sideways(l1, r1)
    l0, r0 = local(functools.partial(bands_kernel, N), [(band, BF16)] * 2, [VM] * 2)(mz, in_z)
    a0 = sideways(l0, r0)
    a2 = sideways(l2, r2)
    half = (2, 2, H, N)
    ez2, oz = local(functools.partial(update_kernel, 0, 1), [(strip, BF16), (half, F32)], [VM] * 6)(
        mz, in_z, obj, ez, *a0)
    hz = swapped(ez2, 1)
    ec2, oc = local(functools.partial(update_kernel, 1, 2), [(strip, BF16), (half, F32)], [VM] * 8)(
        mc, in_c, obj, ec, *a1, *a2)
    hc = swapped(ec2, 0)
    rim_z, rim_c, mz, mc = slots(cnt, pos, ez2, ec2, hz, hc, probe, amps, tab)

    in_c = swapped(rim_c, 0)
    in_z = swapped(rim_z, 1)
    lc, rc = local(functools.partial(bands_kernel, H), [(cut, BF16)] * 2, [VM] * 2)(mc, in_c)
    ac = sideways(lc, rc)
    lz, rz = local(functools.partial(bands_kernel, H), [(cut, BF16)] * 2, [VM] * 2)(mz, in_z)
    az = sideways(lz, rz)
    (out,) = local(finish_kernel, [((2, 2, N, N), F32)], [VM] * 10)(
        mz, in_z, oz, *az, mc, in_c, oc, *ac)
    return out


def solution(mesh):
    return jax.shard_map(
        program,
        mesh=mesh,
        in_specs=(P(None, None, "row", "col"), P(), P("row", "col", None, None), P("row", "col"),
                  P("row", "col", None, None, None)),
        out_specs=P(None, None, "row", "col"),
        check_vma=False,
    )
```

time: 166 us -> 146 us (0.88)
  the two profiles are of different devices: /device:TPU:20 before, /device:TPU:14 now
where the time goes in v2:
time: 146 us; the launch traced here: 145 us
  starting transfers between devices  75.5 us (52%)
  waiting for transfers between devices  50.9 us (35%)
  Pallas kernels  16.4 us (11%)
    ppermute x14, starting transfers between devices, moved(): lax.ppermute(value, axis, [(i, i + steps) for i in range(first, last)])  57.1 us
    ppermute x8, waiting for transfers between devices, swapped(): return lax.ppermute(value, 'row', pairs + [(j, i) for i, j in pairs])  35.6 us
    ppermute x8, starting transfers between devices, swapped(): return lax.ppermute(value, 'row', pairs + [(j, i) for i, j in pairs])  18.3 us
    ppermute x14, waiting for transfers between devices, moved(): lax.ppermute(value, axis, [(i, i + steps) for i in range(first, last)])  15.3 us
    pallas_call x2, Pallas kernels, slots(): local(functools.partial(slots_kernel, LM, RM, RC), [(s, BF16), (s, BF16),...  13.8 us
  transfers between devices with their start and end apart: 22, of which 8 were waited for; matrix products, arithmetic and copies ran while one was open for 0% of the time, Pallas kernels for 1%

profile of v2, /device:TPU:14, one launch (start us, length us, event | category | flops | bytes accessed | tf_op | source)
XLA Modules:
  0.0 145.1 jit_solution(2375286166720669394)
XLA Ops:
  1.3 3.9 %collective-permute-start = (bf16[2,2,128,128]{3,2,1,0:T(8,128)(2,1)S(1)}, bf16[2,2,128,128]{3,2,1,0:T(8,128)(2,1)S(1)}, u32[]{:S(2)}, u32[]{:S(2)}) collective-permute-start(bf16[2,2,128,128]{3,2,1,0:T(8,128)(2,1)S(1)} %get-tuple-element.31), channel_id=1, source_target_pairs={{0,1},{1,2},{2,3},{3,4},{4,5},{5,6},{6,7},{8,9},{9,10},{10,11},{11... | collective-permute-start | bytes 393224 | tf_op jit(solution)/shard_map/ppermute | solution.py:269
  5.2 2.1 %collective-permute-start.1 = (bf16[2,2,128,128]{3,2,1,0:T(8,128)(2,1)S(1)}, bf16[2,2,128,128]{3,2,1,0:T(8,128)(2,1)S(1)}, u32[]{:S(2)}, u32[]{:S(2)}) collective-permute-start(bf16[2,2,128,128]{3,2,1,0:T(8,128)(2,1)S(1)} %get-tuple-element.32), channel_id=1, source_target_pairs={{1,0},{2,1},{3,2},{4,3},{5,4},{6,5},{7,6},{9,8},{10,9},{11,10},{12... | collective-permute-start | bytes 393224 | tf_op jit(solution)/shard_map/ppermute | solution.py:269
  7.3 4.6 %collective-permute-start.2 = (bf16[2,2,128,128]{3,2,1,0:T(8,128)(2,1)S(1)}, bf16[2,2,128,128]{3,2,1,0:T(8,128)(2,1)S(1)}, u32[]{:S(2)}, u32[]{:S(2)}) collective-permute-start(bf16[2,2,128,128]{3,2,1,0:T(8,128)(2,1)S(1)} %get-tuple-element.33), channel_id=1, source_target_pairs={{0,1},{1,2},{2,3},{3,4},{4,5},{5,6},{6,7},{8,9},{9,10},{10,11},{11... | collective-permute-start | bytes 393224 | tf_op jit(solution)/shard_map/ppermute | solution.py:269
  12.0 1.9 %collective-permute-start.3 = (bf16[2,2,128,128]{3,2,1,0:T(8,128)(2,1)S(1)}, bf16[2,2,128,128]{3,2,1,0:T(8,128)(2,1)S(1)}, u32[]{:S(2)}, u32[]{:S(2)}) collective-permute-start(bf16[2,2,128,128]{3,2,1,0:T(8,128)(2,1)S(1)} %get-tuple-element.34), channel_id=1, source_target_pairs={{1,0},{2,1},{3,2},{4,3},{5,4},{6,5},{7,6},{9,8},{10,9},{11,10},{12... | collective-permute-start | bytes 393224 | tf_op jit(solution)/shard_map/ppermute | solution.py:269
  14.0 7.0 %collective-permute-start.4 = (bf16[2,2,128,512]{3,2,1,0:T(8,128)(2,1)S(1)}, bf16[2,2,128,512]{3,2,1,0:T(8,128)(2,1)S(1)}, u32[]{:S(2)}, u32[]{:S(2)}) collective-permute-start(bf16[2,2,128,512]{3,2,1,0:T(8,128)(2,1)S(1)} %shard_map.65.ez.e), channel_id=1, source_target_pairs={{8,16},{24,32},{40,48},{56,64},{72,80},{88,96},{104,112},{120,128}... | collective-permute-start | bytes 1572872 | tf_op jit(solution)/shard_map/ppermute | solution.py:275
  22.2 6.1 %collective-permute-done.4.hz = bf16[2,2,128,512]{3,2,1,0:T(8,128)(2,1)S(1)} collective-permute-done((bf16[2,2,128,512]{3,2,1,0:T(8,128)(2,1)S(1)}, bf16[2,2,128,512]{3,2,1,0:T(8,128)(2,1)S(1)}, u32[]{:S(2)}, u32[]{:S(2)}) %collective-permute-start.4) | collective-permute-done | bytes 524320 | tf_op jit(solution)/shard_map/ppermute | solution.py:275
  28.3 7.1 %shard_map.68 = (bf16[2,2,128,512]{3,2,1,0:T(8,128)(2,1)S(1)}, bf16[2,2,128,512]{3,2,1,0:T(8,128)(2,1)S(1)}, f32[2,2,128,512]{3,2,1,0:T(8,128)S(1)}, f32[2,2,128,512]{3,2,1,0:T(8,128)S(1)}) custom-call(s32[1]{0:T(128)} %bitcast.3.cnt, s32[6,2]{1,0:T(8,128)S(1)} %copy.8.pos, bf16[2,2,128,512]{3,2,1,0:T(8,128)(2,1)S(1)} %shard_map.65.ez.e, ...), custom_call_target="tpu_custom_call" | custom-call | flops 8589934592 | bytes 1048576 | tf_op jit(solution)/shard_map/pallas_call | solution.py:179
  35.5 7.1 %collective-permute-start.6 = (bf16[2,2,128,512]{3,2,1,0:T(8,128)(2,1)S(1)}, bf16[2,2,128,512]{3,2,1,0:T(8,128)(2,1)S(1)}, u32[]{:S(2)}, u32[]{:S(2)}) collective-permute-start(bf16[2,2,128,512]{3,2,1,0:T(8,128)(2,1)S(1)} %get-tuple-element.36), channel_id=1, source_target_pairs={{8,16},{24,32},{40,48},{56,64},{72,80},{88,96},{104,112},{120,128}... | collective-permute-start | bytes 1572872 | tf_op jit(solution)/shard_map/ppermute | solution.py:275
  42.7 1.9 %collective-permute-start.10 = (bf16[2,2,64,256]{3,2,1,0:T(8,128)(2,1)S(1)}, bf16[2,2,64,256]{3,2,1,0:T(8,128)(2,1)S(1)}, u32[]{:S(2)}, u32[]{:S(2)}) collective-permute-start(bf16[2,2,64,256]{3,2,1,0:T(8,128)(2,1)S(1)} %get-tuple-element.42), channel_id=1, source_target_pairs={{0,1},{1,2},{2,3},{3,4},{4,5},{5,6},{6,7},{8,9},{9,10},{10,11},{11... | collective-permute-start | bytes 393224 | tf_op jit(solution)/shard_map/ppermute | solution.py:269
  44.7 5.2 %collective-permute-done.6.rim = bf16[2,2,128,512]{3,2,1,0:T(8,128)(2,1)S(1)} collective-permute-done((bf16[2,2,128,512]{3,2,1,0:T(8,128)(2,1)S(1)}, bf16[2,2,128,512]{3,2,1,0:T(8,128)(2,1)S(1)}, u32[]{:S(2)}, u32[]{:S(2)}) %collective-permute-start.6) | collective-permute-done | bytes 524320 | tf_op jit(solution)/shard_map/ppermute | solution.py:275
  50.0 4.8 %collective-permute-start.7 = (bf16[2,2,128,256]{3,2,1,0:T(8,128)(2,1)S(1)}, bf16[2,2,128,256]{3,2,1,0:T(8,128)(2,1)S(1)}, u32[]{:S(2)}, u32[]{:S(2)}) collective-permute-start(bf16[2,2,128,256]{3,2,1,0:T(8,128)(2,1)S(1)} %get-tuple-element.37), channel_id=1, source_target_pairs={{0,1},{1,2},{2,3},{3,4},{4,5},{5,6},{6,7},{8,9},{9,10},{10,11},{11... | collective-permute-start | bytes 786440 | tf_op jit(solution)/shard_map/ppermute | solution.py:269
  54.8 1.9 %collective-permute-start.8 = (bf16[2,2,128,256]{3,2,1,0:T(8,128)(2,1)S(1)}, bf16[2,2,128,256]{3,2,1,0:T(8,128)(2,1)S(1)}, u32[]{:S(2)}, u32[]{:S(2)}) collective-permute-start(bf16[2,2,128,256]{3,2,1,0:T(8,128)(2,1)S(1)} %get-tuple-element.38), channel_id=1, source_target_pairs={{1,0},{2,1},{3,2},{4,3},{5,4},{6,5},{7,6},{9,8},{10,9},{11,10},{12... | collective-permute-start | bytes 786440 | tf_op jit(solution)/shard_map/ppermute | solution.py:269
  56.7 8.5 %collective-permute-start.11 = (bf16[2,2,64,256]{3,2,1,0:T(8,128)(2,1)S(1)}, bf16[2,2,64,256]{3,2,1,0:T(8,128)(2,1)S(1)}, u32[]{:S(2)}, u32[]{:S(2)}) collective-permute-start(bf16[2,2,64,256]{3,2,1,0:T(8,128)(2,1)S(1)} %get-tuple-element.43), channel_id=1, source_target_pairs={{1,0},{2,1},{3,2},{4,3},{5,4},{6,5},{7,6},{9,8},{10,9},{11,10},{12... | collective-permute-start | bytes 393224 | tf_op jit(solution)/shard_map/ppermute | solution.py:269
  65.3 5.3 %collective-permute-start.12 = (bf16[2,2,64,256]{3,2,1,0:T(8,128)(2,1)S(1)}, bf16[2,2,64,256]{3,2,1,0:T(8,128)(2,1)S(1)}, u32[]{:S(2)}, u32[]{:S(2)}) collective-permute-start(bf16[2,2,64,256]{3,2,1,0:T(8,128)(2,1)S(1)} %get-tuple-element.44), channel_id=1, source_target_pairs={{0,1},{1,2},{2,3},{3,4},{4,5},{5,6},{6,7},{8,9},{9,10},{10,11},{11... | collective-permute-start | bytes 393224 | tf_op jit(solution)/shard_map/ppermute | solution.py:269
  72.5 6.6 %collective-permute-done.11.rest_1_ = bf16[2,2,64,256]{3,2,1,0:T(8,128)(2,1)S(1)} collective-permute-done((bf16[2,2,64,256]{3,2,1,0:T(8,128)(2,1)S(1)}, bf16[2,2,64,256]{3,2,1,0:T(8,128)(2,1)S(1)}, u32[]{:S(2)}, u32[]{:S(2)}) %collective-permute-start.11) | collective-permute-done | bytes 131104 | tf_op jit(solution)/shard_map/ppermute | solution.py:269
  79.2 2.8 %collective-permute-done.13.rest_3_ = bf16[2,2,64,256]{3,2,1,0:T(8,128)(2,1)S(1)} collective-permute-done((bf16[2,2,64,256]{3,2,1,0:T(8,128)(2,1)S(1)}, bf16[2,2,64,256]{3,2,1,0:T(8,128)(2,1)S(1)}, u32[]{:S(2)}, u32[]{:S(2)}) %collective-permute-start.13) | collective-permute-done | bytes 131104 | tf_op jit(solution)/shard_map/ppermute | solution.py:269
  84.6 12.2 %collective-permute-done.14.hz = bf16[2,2,128,512]{3,2,1,0:T(8,128)(2,1)S(1)} collective-permute-done((bf16[2,2,128,512]{3,2,1,0:T(8,128)(2,1)S(1)}, bf16[2,2,128,512]{3,2,1,0:T(8,128)(2,1)S(1)}, u32[]{:S(2)}, u32[]{:S(2)}) %collective-permute-start.14) | collective-permute-done | bytes 524320 | tf_op jit(solution)/shard_map/ppermute | solution.py:275
  96.8 6.7 %shard_map.73 = (bf16[2,2,128,512]{3,2,1,0:T(8,128)(2,1)S(1)}, bf16[2,2,128,512]{3,2,1,0:T(8,128)(2,1)S(1)}, f32[2,2,128,512]{3,2,1,0:T(8,128)S(1)}, f32[2,2,128,512]{3,2,1,0:T(8,128)S(1)}) custom-call(s32[1]{0:T(128)} %bitcast.4.cnt, s32[6,2]{1,0:T(8,128)S(1)} %copy.8.pos, bf16[2,2,128,512]{3,2,1,0:T(8,128)(2,1)S(1)} %get-tuple-element.39.ez, ...), custom_call_target="tpu_custom_call" | custom-call | flops 8589934592 | bytes 1048576 | tf_op jit(solution)/shard_map/pallas_call | solution.py:179
  103.5 1.9 %collective-permute-start.16 = (bf16[2,2,128,512]{3,2,1,0:T(8,128)(2,1)S(1)}, bf16[2,2,128,512]{3,2,1,0:T(8,128)(2,1)S(1)}, u32[]{:S(2)}, u32[]{:S(2)}) collective-permute-start(bf16[2,2,128,512]{3,2,1,0:T(8,128)(2,1)S(1)} %get-tuple-element.48), channel_id=1, source_target_pairs={{8,16},{24,32},{40,48},{56,64},{72,80},{88,96},{104,112},{120,128}... | collective-permute-start | bytes 1572872 | tf_op jit(solution)/shard_map/ppermute | solution.py:275
  105.5 12.2 %collective-permute-done.16.rim.rimz = bf16[2,2,128,512]{3,2,1,0:T(8,128)(2,1)S(1)} collective-permute-done((bf16[2,2,128,512]{3,2,1,0:T(8,128)(2,1)S(1)}, bf16[2,2,128,512]{3,2,1,0:T(8,128)(2,1)S(1)}, u32[]{:S(2)}, u32[]{:S(2)}) %collective-permute-start.16) | collective-permute-done | bytes 524320 | tf_op jit(solution)/shard_map/ppermute | solution.py:275
  117.8 2.8 %collective-permute-start.17 = (bf16[2,2,128,128]{3,2,1,0:T(8,128)(2,1)S(1)}, bf16[2,2,128,128]{3,2,1,0:T(8,128)(2,1)S(1)}, u32[]{:S(2)}, u32[]{:S(2)}) collective-permute-start(bf16[2,2,128,128]{3,2,1,0:T(8,128)(2,1)S(1)} %get-tuple-element.50), channel_id=1, source_target_pairs={{0,1},{1,2},{2,3},{3,4},{4,5},{5,6},{6,7},{8,9},{9,10},{10,11},{11... | collective-permute-start | bytes 393224 | tf_op jit(solution)/shard_map/ppermute | solution.py:269
  120.5 3.1 %collective-permute-start.18 = (bf16[2,2,128,128]{3,2,1,0:T(8,128)(2,1)S(1)}, bf16[2,2,128,128]{3,2,1,0:T(8,128)(2,1)S(1)}, u32[]{:S(2)}, u32[]{:S(2)}) collective-permute-start(bf16[2,2,128,128]{3,2,1,0:T(8,128)(2,1)S(1)} %get-tuple-element.51), channel_id=1, source_target_pairs={{1,0},{2,1},{3,2},{4,3},{5,4},{6,5},{7,6},{9,8},{10,9},{11,10},{12... | collective-permute-start | bytes 393224 | tf_op jit(solution)/shard_map/ppermute | solution.py:269
  123.7 12.4 %collective-permute-start.20 = (bf16[2,2,128,128]{3,2,1,0:T(8,128)(2,1)S(1)}, bf16[2,2,128,128]{3,2,1,0:T(8,128)(2,1)S(1)}, u32[]{:S(2)}, u32[]{:S(2)}) collective-permute-start(bf16[2,2,128,128]{3,2,1,0:T(8,128)(2,1)S(1)} %get-tuple-element.55), channel_id=1, source_target_pairs={{0,1},{1,2},{2,3},{3,4},{4,5},{5,6},{6,7},{8,9},{9,10},{10,11},{11... | collective-permute-start | bytes 393224 | tf_op jit(solution)/shard_map/ppermute | solution.py:269
  138.6 5.3 %collective-permute-done.21.rc = bf16[2,2,128,128]{3,2,1,0:T(8,128)(2,1)S(1)} collective-permute-done((bf16[2,2,128,128]{3,2,1,0:T(8,128)(2,1)S(1)}, bf16[2,2,128,128]{3,2,1,0:T(8,128)(2,1)S(1)}, u32[]{:S(2)}, u32[]{:S(2)}) %collective-permute-start.21) | collective-permute-done | bytes 131104 | tf_op jit(solution)/shard_map/ppermute | solution.py:269
  (46 shorter events, 10.7 us)
Async XLA Ops:
  1.3 20.7 %copy-start.2 = (bf16[4,256,256]{2,1,0:T(8,128)(2,1)S(1)}, bf16[4,256,256]{2,1,0:T(8,128)(2,1)}, u32[]{:S(2)}) copy-start(bf16[4,256,256]{2,1,0:T(8,128)(2,1)} %constant.2.clone.base) | copy-start | bytes 1572868
  1.3 12.6 %collective-permute-start = (bf16[2,2,128,128]{3,2,1,0:T(8,128)(2,1)S(1)}, bf16[2,2,128,128]{3,2,1,0:T(8,128)(2,1)S(1)}, u32[]{:S(2)}, u32[]{:S(2)}) collective-permute-start(bf16[2,2,128,128]{3,2,1,0:T(8,128)(2,1)S(1)} %get-tuple-element.31), channel_id=1, source_target_pairs={{0,1},{1,2},{2,3},{3,4},{4,5},{5,6},{6,7},{8,9},{9,10},{10,11},{11... | collective-permute-start | bytes 393224 | tf_op jit(solution)/shard_map/ppermute | solution.py:269
  5.2 8.7 %collective-permute-start.1 = (bf16[2,2,128,128]{3,2,1,0:T(8,128)(2,1)S(1)}, bf16[2,2,128,128]{3,2,1,0:T(8,128)(2,1)S(1)}, u32[]{:S(2)}, u32[]{:S(2)}) collective-permute-start(bf16[2,2,128,128]{3,2,1,0:T(8,128)(2,1)S(1)} %get-tuple-element.32), channel_id=1, source_target_pairs={{1,0},{2,1},{3,2},{4,3},{5,4},{6,5},{7,6},{9,8},{10,9},{11,10},{12... | collective-permute-start | bytes 393224 | tf_op jit(solution)/shard_map/ppermute | solution.py:269
  7.3 13.8 %collective-permute-start.2 = (bf16[2,2,128,128]{3,2,1,0:T(8,128)(2,1)S(1)}, bf16[2,2,128,128]{3,2,1,0:T(8,128)(2,1)S(1)}, u32[]{:S(2)}, u32[]{:S(2)}) collective-permute-start(bf16[2,2,128,128]{3,2,1,0:T(8,128)(2,1)S(1)} %get-tuple-element.33), channel_id=1, source_target_pairs={{0,1},{1,2},{2,3},{3,4},{4,5},{5,6},{6,7},{8,9},{9,10},{10,11},{11... | collective-permute-start | bytes 393224 | tf_op jit(solution)/shard_map/ppermute | solution.py:269
  12.0 9.1 %collective-permute-start.3 = (bf16[2,2,128,128]{3,2,1,0:T(8,128)(2,1)S(1)}, bf16[2,2,128,128]{3,2,1,0:T(8,128)(2,1)S(1)}, u32[]{:S(2)}, u32[]{:S(2)}) collective-permute-start(bf16[2,2,128,128]{3,2,1,0:T(8,128)(2,1)S(1)} %get-tuple-element.34), channel_id=1, source_target_pairs={{1,0},{2,1},{3,2},{4,3},{5,4},{6,5},{7,6},{9,8},{10,9},{11,10},{12... | collective-permute-start | bytes 393224 | tf_op jit(solution)/shard_map/ppermute | solution.py:269
  14.0 14.2 %collective-permute-start.4 = (bf16[2,2,128,512]{3,2,1,0:T(8,128)(2,1)S(1)}, bf16[2,2,128,512]{3,2,1,0:T(8,128)(2,1)S(1)}, u32[]{:S(2)}, u32[]{:S(2)}) collective-permute-start(bf16[2,2,128,512]{3,2,1,0:T(8,128)(2,1)S(1)} %shard_map.65.ez.e), channel_id=1, source_target_pairs={{8,16},{24,32},{40,48},{56,64},{72,80},{88,96},{104,112},{120,128}... | collective-permute-start | bytes 1572872 | tf_op jit(solution)/shard_map/ppermute | solution.py:275
  21.2 7.1 %collective-permute-start.5 = (bf16[2,2,128,512]{3,2,1,0:T(8,128)(2,1)S(1)}, bf16[2,2,128,512]{3,2,1,0:T(8,128)(2,1)}, u32[]{:S(2)}, u32[]{:S(2)}) collective-permute-start(bf16[2,2,128,512]{3,2,1,0:T(8,128)(2,1)S(1)} %shard_map.66.ec.e), channel_id=1, source_target_pairs={{0,8},{16,24},{32,40},{48,56},{64,72},{80,88},{96,104},{112,120},{... | collective-permute-start | bytes 1572872 | tf_op jit(solution)/shard_map/ppermute | solution.py:275
  35.4 46.6 %copy-start.1 = (f32[2,2,256,256]{3,2,1,0:T(8,128)S(1)}, f32[2,2,256,256]{3,2,1,0:T(8,128)}, u32[]{:S(2)}) copy-start(f32[2,2,256,256]{3,2,1,0:T(8,128)} %obj.9) | copy-start | bytes 3145732
  35.4 7.2 %collective-permute-start.9 = (bf16[2,2,128,512]{3,2,1,0:T(8,128)(2,1)S(1)}, bf16[2,2,128,512]{3,2,1,0:T(8,128)(2,1)S(1)}, u32[]{:S(2)}, u32[]{:S(2)}) collective-permute-start(bf16[2,2,128,512]{3,2,1,0:T(8,128)(2,1)S(1)} %get-tuple-element.41), channel_id=1, source_target_pairs={{0,8},{16,24},{32,40},{48,56},{64,72},{80,88},{96,104},{112,120},{... | collective-permute-start | bytes 1572872 | tf_op jit(solution)/shard_map/ppermute | solution.py:275
  35.5 14.3 %collective-permute-start.6 = (bf16[2,2,128,512]{3,2,1,0:T(8,128)(2,1)S(1)}, bf16[2,2,128,512]{3,2,1,0:T(8,128)(2,1)S(1)}, u32[]{:S(2)}, u32[]{:S(2)}) collective-permute-start(bf16[2,2,128,512]{3,2,1,0:T(8,128)(2,1)S(1)} %get-tuple-element.36), channel_id=1, source_target_pairs={{8,16},{24,32},{40,48},{56,64},{72,80},{88,96},{104,112},{120,128}... | collective-permute-start | bytes 1572872 | tf_op jit(solution)/shard_map/ppermute | solution.py:275
  42.7 27.9 %collective-permute-start.10 = (bf16[2,2,64,256]{3,2,1,0:T(8,128)(2,1)S(1)}, bf16[2,2,64,256]{3,2,1,0:T(8,128)(2,1)S(1)}, u32[]{:S(2)}, u32[]{:S(2)}) collective-permute-start(bf16[2,2,64,256]{3,2,1,0:T(8,128)(2,1)S(1)} %get-tuple-element.42), channel_id=1, source_target_pairs={{0,1},{1,2},{2,3},{3,4},{4,5},{5,6},{6,7},{8,9},{9,10},{10,11},{11... | collective-permute-start | bytes 393224 | tf_op jit(solution)/shard_map/ppermute | solution.py:269
  50.0 32.4 %collective-permute-start.7 = (bf16[2,2,128,256]{3,2,1,0:T(8,128)(2,1)S(1)}, bf16[2,2,128,256]{3,2,1,0:T(8,128)(2,1)S(1)}, u32[]{:S(2)}, u32[]{:S(2)}) collective-permute-start(bf16[2,2,128,256]{3,2,1,0:T(8,128)(2,1)S(1)} %get-tuple-element.37), channel_id=1, source_target_pairs={{0,1},{1,2},{2,3},{3,4},{4,5},{5,6},{6,7},{8,9},{9,10},{10,11},{11... | collective-permute-start | bytes 786440 | tf_op jit(solution)/shard_map/ppermute | solution.py:269
  54.8 27.6 %collective-permute-start.8 = (bf16[2,2,128,256]{3,2,1,0:T(8,128)(2,1)S(1)}, bf16[2,2,128,256]{3,2,1,0:T(8,128)(2,1)S(1)}, u32[]{:S(2)}, u32[]{:S(2)}) collective-permute-start(bf16[2,2,128,256]{3,2,1,0:T(8,128)(2,1)S(1)} %get-tuple-element.38), channel_id=1, source_target_pairs={{1,0},{2,1},{3,2},{4,3},{5,4},{6,5},{7,6},{9,8},{10,9},{11,10},{12... | collective-permute-start | bytes 786440 | tf_op jit(solution)/shard_map/ppermute | solution.py:269
  56.7 22.4 %collective-permute-start.11 = (bf16[2,2,64,256]{3,2,1,0:T(8,128)(2,1)S(1)}, bf16[2,2,64,256]{3,2,1,0:T(8,128)(2,1)S(1)}, u32[]{:S(2)}, u32[]{:S(2)}) collective-permute-start(bf16[2,2,64,256]{3,2,1,0:T(8,128)(2,1)S(1)} %get-tuple-element.43), channel_id=1, source_target_pairs={{1,0},{2,1},{3,2},{4,3},{5,4},{6,5},{7,6},{9,8},{10,9},{11,10},{12... | collective-permute-start | bytes 393224 | tf_op jit(solution)/shard_map/ppermute | solution.py:269
  65.3 13.9 %collective-permute-start.12 = (bf16[2,2,64,256]{3,2,1,0:T(8,128)(2,1)S(1)}, bf16[2,2,64,256]{3,2,1,0:T(8,128)(2,1)S(1)}, u32[]{:S(2)}, u32[]{:S(2)}) collective-permute-start(bf16[2,2,64,256]{3,2,1,0:T(8,128)(2,1)S(1)} %get-tuple-element.44), channel_id=1, source_target_pairs={{0,1},{1,2},{2,3},{3,4},{4,5},{5,6},{6,7},{8,9},{9,10},{10,11},{11... | collective-permute-start | bytes 393224 | tf_op jit(solution)/shard_map/ppermute | solution.py:269
  70.6 11.4 %collective-permute-start.13 = (bf16[2,2,64,256]{3,2,1,0:T(8,128)(2,1)S(1)}, bf16[2,2,64,256]{3,2,1,0:T(8,128)(2,1)S(1)}, u32[]{:S(2)}, u32[]{:S(2)}) collective-permute-start(bf16[2,2,64,256]{3,2,1,0:T(8,128)(2,1)S(1)} %get-tuple-element.45), channel_id=1, source_target_pairs={{1,0},{2,1},{3,2},{4,3},{5,4},{6,5},{7,6},{9,8},{10,9},{11,10},{12... | collective-permute-start | bytes 393224 | tf_op jit(solution)/shard_map/ppermute | solution.py:269
  82.3 2.4 %collective-permute-start.15 = (bf16[2,2,128,512]{3,2,1,0:T(8,128)(2,1)S(1)}, bf16[2,2,128,512]{3,2,1,0:T(8,128)(2,1)S(1)}, u32[]{:S(2)}, u32[]{:S(2)}) collective-permute-start(bf16[2,2,128,512]{3,2,1,0:T(8,128)(2,1)S(1)} %get-tuple-element.46.ec), channel_id=1, source_target_pairs={{0,8},{16,24},{32,40},{48,56},{64,72},{80,88},{96,104},{112,120},{... | collective-permute-start | bytes 1572872 | tf_op jit(solution)/shard_map/ppermute | solution.py:275
  82.7 14.1 %collective-permute-start.14 = (bf16[2,2,128,512]{3,2,1,0:T(8,128)(2,1)S(1)}, bf16[2,2,128,512]{3,2,1,0:T(8,128)(2,1)S(1)}, u32[]{:S(2)}, u32[]{:S(2)}) collective-permute-start(bf16[2,2,128,512]{3,2,1,0:T(8,128)(2,1)S(1)} %get-tuple-element.39.ez), channel_id=1, source_target_pairs={{8,16},{24,32},{40,48},{56,64},{72,80},{88,96},{104,112},{120,128}... | collective-permute-start | bytes 1572872 | tf_op jit(solution)/shard_map/ppermute | solution.py:275
  103.5 14.2 %collective-permute-start.16 = (bf16[2,2,128,512]{3,2,1,0:T(8,128)(2,1)S(1)}, bf16[2,2,128,512]{3,2,1,0:T(8,128)(2,1)S(1)}, u32[]{:S(2)}, u32[]{:S(2)}) collective-permute-start(bf16[2,2,128,512]{3,2,1,0:T(8,128)(2,1)S(1)} %get-tuple-element.48), channel_id=1, source_target_pairs={{8,16},{24,32},{40,48},{56,64},{72,80},{88,96},{104,112},{120,128}... | collective-permute-start | bytes 1572872 | tf_op jit(solution)/shard_map/ppermute | solution.py:275
  105.4 18.2 %collective-permute-start.19 = (bf16[2,2,128,512]{3,2,1,0:T(8,128)(2,1)S(1)}, bf16[2,2,128,512]{3,2,1,0:T(8,128)(2,1)S(1)}, u32[]{:S(2)}, u32[]{:S(2)}) collective-permute-start(bf16[2,2,128,512]{3,2,1,0:T(8,128)(2,1)S(1)} %get-tuple-element.53), channel_id=1, source_target_pairs={{0,8},{16,24},{32,40},{48,56},{64,72},{80,88},{96,104},{112,120},{... | collective-permute-start | bytes 1572872 | tf_op jit(solution)/shard_map/ppermute | solution.py:275
  117.8 20.3 %collective-permute-start.17 = (bf16[2,2,128,128]{3,2,1,0:T(8,128)(2,1)S(1)}, bf16[2,2,128,128]{3,2,1,0:T(8,128)(2,1)S(1)}, u32[]{:S(2)}, u32[]{:S(2)}) collective-permute-start(bf16[2,2,128,128]{3,2,1,0:T(8,128)(2,1)S(1)} %get-tuple-element.50), channel_id=1, source_target_pairs={{0,1},{1,2},{2,3},{3,4},{4,5},{5,6},{6,7},{8,9},{9,10},{10,11},{11... | collective-permute-start | bytes 393224 | tf_op jit(solution)/shard_map/ppermute | solution.py:269
  120.5 17.5 %collective-permute-start.18 = (bf16[2,2,128,128]{3,2,1,0:T(8,128)(2,1)S(1)}, bf16[2,2,128,128]{3,2,1,0:T(8,128)(2,1)S(1)}, u32[]{:S(2)}, u32[]{:S(2)}) collective-permute-start(bf16[2,2,128,128]{3,2,1,0:T(8,128)(2,1)S(1)} %get-tuple-element.51), channel_id=1, source_target_pairs={{1,0},{2,1},{3,2},{4,3},{5,4},{6,5},{7,6},{9,8},{10,9},{11,10},{12... | collective-permute-start | bytes 393224 | tf_op jit(solution)/shard_map/ppermute | solution.py:269
  123.7 14.9 %collective-permute-start.20 = (bf16[2,2,128,128]{3,2,1,0:T(8,128)(2,1)S(1)}, bf16[2,2,128,128]{3,2,1,0:T(8,128)(2,1)S(1)}, u32[]{:S(2)}, u32[]{:S(2)}) collective-permute-start(bf16[2,2,128,128]{3,2,1,0:T(8,128)(2,1)S(1)} %get-tuple-element.55), channel_id=1, source_target_pairs={{0,1},{1,2},{2,3},{3,4},{4,5},{5,6},{6,7},{8,9},{9,10},{10,11},{11... | collective-permute-start | bytes 393224 | tf_op jit(solution)/shard_map/ppermute | solution.py:269
  136.1 7.8 %collective-permute-start.21 = (bf16[2,2,128,128]{3,2,1,0:T(8,128)(2,1)S(1)}, bf16[2,2,128,128]{3,2,1,0:T(8,128)(2,1)S(1)}, u32[]{:S(2)}, u32[]{:S(2)}) collective-permute-start(bf16[2,2,128,128]{3,2,1,0:T(8,128)(2,1)S(1)} %get-tuple-element.56), channel_id=1, source_target_pairs={{1,0},{2,1},{3,2},{4,3},{5,4},{6,5},{7,6},{9,8},{10,9},{11,10},{12... | collective-permute-start | bytes 393224 | tf_op jit(solution)/shard_map/ppermute | solution.py:269
  (4 other events, 50.4 us)

commit v3 on v2

v3 whole, which is shorter than its diff:
```python
import functools
import jax, jax.numpy as jnp
from jax import lax
import numpy as np
from jax.experimental import pallas as pl
from jax.experimental.pallas import tpu as pltpu
from jax.sharding import PartitionSpec as P

RATE = 0.1
H = 128
FEW = 32

N = 256
F32, BF16 = jnp.float32, jnp.bfloat16


def tables():
    k = np.arange(N)
    ang = 2 * np.pi * ((k[:, None] * k[None, :]) % N) / N
    f = np.exp(-1j * ang) / 16.0
    fk = np.where(k < N // 2, k, k - N).astype(np.float64)
    ker = (np.exp(-1j * np.pi * fk * fk / (2 * N))[None, :] * np.exp(1j * ang)).sum(1) / N
    p = ker[(k[:, None] - k[None, :]) % N]

    return np.stack([f.real, f.imag, p.real, p.imag]).astype(jnp.bfloat16)


def dot(a, b):
    return jnp.dot(a, b, preferred_element_type=F32)


def body(j, y, x, refs, LM, RM, RC):
    ext, grad, xs, yh, mid, sec, probe, amps, tab = refs
    q = x // 128
    s = x - q * 128
    back = (128 - s) % 128

    def lanes(rows):
        return lax.broadcasted_iota(jnp.int32, (rows, 128), 1)

    def window(p, r0, rows):
        parts = [pltpu.roll(ext[p, q + t, pl.ds(y + r0, rows), :], back, 1) for t in range(3)]
        keep = lanes(rows) < 128 - s
        return [jnp.where(keep, parts[t], parts[t + 1]) for t in range(2)]

    def cut(i, _):
        r0 = pl.multiple_of(i * RC, RC)
        wr, wi = window(0, r0, RC), window(1, r0, RC)
        sr, si = window(2, r0, RC), window(3, r0, RC)
        for t in range(2):
            cols = pl.ds(128 * t, 128)
            pr, pi = probe[0, pl.ds(r0, RC), cols], probe[1, pl.ds(r0, RC), cols]
            fr, fi = 1.0 + wr[t], wi[t]
            xs[pl.ds(r0, RC), cols] = (pr * fr - pi * fi).astype(BF16)
            xs[pl.ds(N + r0, RC), cols] = (pr * fi + pi * fr).astype(BF16)
            sec[0, pl.ds(r0, RC), cols] = 1.0 + sr[t]
            sec[1, pl.ds(r0, RC), cols] = si[t]
        return 0

    lax.fori_loop(0, N // RC, cut, 0, unroll=True)

    def left(m):
        for a in range(0, 2 * N, LM):
            out = dot(tab[m, a:a + LM, :], xs[...]).astype(BF16)
            if LM == 2 * N:
                yh[:, :N] = out[:N]
                yh[:, N:] = out[N:]
            else:
                yh[a % N:a % N + LM, (a // N) * N:(a // N) * N + N] = out

    def right(m, use):
        for a in range(0, N, RM):
            z = dot(yh[a:a + RM, :], tab[m, :, :])
            use(slice(a, a + RM), z[:, :N], z[:, N:])

    def put(rs, zr, zi):
        mr, mi = zr.astype(BF16), zi.astype(BF16)
        mid[0, rs, :] = mr
        mid[1, rs, :] = mi
        mr, mi = mr.astype(F32), mi.astype(F32)
        sr, si = sec[0, rs, :], sec[1, rs, :]
        xs[rs, :] = (mr * sr - mi * si).astype(BF16)
        xs[N + rs.start:N + rs.stop, :] = (mr * si + mi * sr).astype(BF16)

    left(2)
    right(3, put)

    def resid(rs, zr, zi):
        a = amps[j, rs, :].astype(F32)
        f = 1.0 - a * lax.rsqrt(zr * zr + zi * zi + 0.25)
        xs[rs, :] = (f * zr).astype(BF16)
        xs[N + rs.start:N + rs.stop, :] = (f * zi).astype(BF16)

    left(0)
    right(1, resid)

    def accumulate(p, rs, g):
        rows = rs.stop - rs.start
        g0, g1 = pltpu.roll(g[:, :128], s, 1), pltpu.roll(g[:, 128:], s, 1)
        hi = lanes(rows) >= s
        zero = jnp.zeros((rows, 128), F32)
        at = pl.ds(y + rs.start, rows)
        grad[p, q, at, :] += jnp.where(hi, g0, zero)
        grad[p, q + 1, at, :] += jnp.where(hi, g1, g0)
        grad[p, q + 2, at, :] += jnp.where(hi, zero, g1)

    def far(rs, zr, zi):
        mr, mi = mid[0, rs, :].astype(F32), mid[1, rs, :].astype(F32)
        accumulate(2, rs, zr * mr + zi * mi)
        accumulate(3, rs, zi * mr - zr * mi)
        sr, si = sec[0, rs, :], sec[1, rs, :]
        xs[rs, :] = (zr * sr + zi * si).astype(BF16)
        xs[N + rs.start:N + rs.stop, :] = (zi * sr - zr * si).astype(BF16)

    left(1)
    right(0, far)

    def near(rs, zr, zi):
        pr, pi = probe[0, rs, :], probe[1, rs, :]
        accumulate(0, rs, zr * pr + zi * pi)
        accumulate(1, rs, zi * pr - zr * pi)

    left(3)
    right(2, near)


PLANES = [(a, b) for a in range(2) for b in range(2)]
VM = pl.BlockSpec(memory_space=pltpu.VMEM)
SM = pl.BlockSpec(memory_space=pltpu.SMEM)


def local(fn, outs, specs, scratch=(), places=None, flops=0, moved=1 << 20, vmem=8 << 20):
    return pl.pallas_call(
        fn,
        out_shape=tuple(jax.ShapeDtypeStruct(s, d) for s, d in outs),
        in_specs=specs,
        out_specs=tuple(places or [VM] * len(outs)),
        scratch_shapes=list(scratch),
        cost_estimate=pl.CostEstimate(flops=flops, bytes_accessed=moved, transcendentals=0),
        compiler_params=pltpu.CompilerParams(vmem_limit_bytes=vmem),
    )


def parity():
    return lax.rem(lax.axis_index("row"), 2)


def block(k):
    return pl.multiple_of(jnp.where(parity() == 0, H * k, H * (3 - k)), H)


def own(k):
    return pl.multiple_of(jnp.where(parity() == k, 0, H), H)


def slots_kernel(LM, RM, RC, scalars, ez, ec, hz, hc, probe, amps, base, rz, rc, mz, mc,
                 ext, grad, xs, yh, mid, sec, tab):
    for m in range(2):
        re, im = base[2 * m], base[2 * m + 1]
        for conj in range(2):
            k = 2 * m + conj
            tab[k, 0:N, 0:N] = re
            tab[k, N:, N:] = re
            tab[k, 0:N, N:] = im if conj else -im
            tab[k, N:, 0:N] = -im if conj else im
    for k, strip in enumerate((hz, ez, ec, hc)):
        at = pl.ds(block(k), H)
        for p, (a, b) in enumerate(PLANES):
            for t in range(4):
                ext[p, t, at, :] = strip[a, b, :, H * t:H * t + H].astype(F32)
    grad[...] = jnp.zeros(grad.shape, F32)
    refs = (ext, grad, xs, yh, mid, sec, probe, amps, tab)

    def step(j, _):
        body(j, scalars[2 * j + 1], scalars[2 * j + 2], refs, LM, RM, RC)
        return 0

    lax.fori_loop(0, scalars[0], step, 0)
    for k, strip in enumerate((rz, mz, mc, rc)):
        at = pl.ds(block(k), H)
        for p, (a, b) in enumerate(PLANES):
            for t in range(4):
                strip[a, b, :, H * t:H * t + H] = grad[p, t, at, :].astype(strip.dtype)


def slots(scalars, ez, ec, hz, hc, probe, amps, base, LM=256, RM=128, RC=32):
    s = (2, 2, H, 512)
    return local(
        functools.partial(slots_kernel, LM, RM, RC),
        [(s, BF16), (s, BF16), (s, F32), (s, F32)],
        [SM] + [VM] * 7,
        [pltpu.VMEM((4, 5, 512, H), F32), pltpu.VMEM((4, 5, 512, H), F32),
         pltpu.VMEM((512, N), BF16), pltpu.VMEM((N, 512), BF16),
         pltpu.VMEM((2, N, N), BF16), pltpu.VMEM((2, N, N), F32),
         pltpu.VMEM((4, 2 * N, 2 * N), BF16)],
        flops=1 << 33, vmem=20 << 20,
    )(scalars, ez, ec, hz, hc, probe, amps, base)


def by_column(run, inner, outer):
    odd = lax.rem(lax.axis_index("col"), 2)
    pl.when(odd == 0)(lambda: run(outer, inner))
    pl.when(odd == 1)(lambda: run(inner, outer))


def setup_kernel(base, pos, cnt, kept, scalars):
    kept[...] = base[...]
    scalars[0] = cnt[0, 0]
    for j in range(6):
        scalars[2 * j + 1] = pos[0, 0, j, 0]
        scalars[2 * j + 2] = pos[0, 0, j, 1]


def edges_kernel(obj, iz, oz, ic, oc):
    def run(left, right):
        for k in range(2):
            at = pl.ds(own(k), H)
            for a, b in PLANES:
                left[k][a, b] = obj[a, b, at, 0:H].astype(BF16)
                right[k][a, b] = obj[a, b, at, N - H:N].astype(BF16)

    by_column(run, (iz, ic), (oz, oc))


def join_kernel(k, obj, inner, outer, e):
    at = pl.ds(own(k), H)

    def run(left, right):
        for a, b in PLANES:
            e[a, b, :, 0:H] = left[a, b]
            e[a, b, :, H:3 * H] = obj[a, b, at, :].astype(BF16)
            e[a, b, :, 3 * H:] = right[a, b]

    by_column(run, inner, outer)


def bands_kernel(width, m, rim, *outs):
    def run(left, right):
        r0 = 0
        for l, r in zip(left, right):
            rs = slice(r0, r0 + l.shape[2])
            for a, b in PLANES:
                l[a, b] = (m[a, b, rs, 0:width] + rim[a, b, rs, 0:width].astype(F32)).astype(BF16)
                r[a, b] = (m[a, b, rs, 512 - width:] + rim[a, b, rs, 512 - width:].astype(F32)).astype(BF16)
            r0 = rs.stop

    by_column(run, outs[0::2], outs[1::2])


def update_kernel(k, chunks, m, rim, obj, e, *rest):
    arrived, (e_new, o_new) = rest[:2 * chunks], rest[2 * chunks:]
    column = lax.axis_index("col")
    keep_left = (column > 0).astype(F32)
    keep_right = (column < lax.axis_size("col") - 1).astype(F32)

    def run(lefts, rights):
        r0 = 0
        for from_left, from_right in zip(lefts, rights):
            rows = from_left.shape[2]
            rs = slice(r0, r0 + rows)
            at = pl.ds(own(k) + r0, rows)
            for a, b in PLANES:
                for side, other, keep in ((0, from_left, keep_left), (1, from_right, keep_right)):
                    cols = slice(N * side, N * side + N)
                    total = RATE * (m[a, b, rs, cols] + rim[a, b, rs, cols].astype(F32) + other[a, b].astype(F32))
                    outside, inside = (slice(0, H), slice(H, N)) if side == 0 else (slice(H, N), slice(0, H))
                    halo = slice(3 * H * side, 3 * H * side + H)
                    mine = slice(H * side, H * side + H)
                    old = e[a, b, rs, halo].astype(F32)
                    e_new[a, b, rs, halo] = (keep * (old - total[:, outside])).astype(BF16)
                    value = obj[a, b, at, mine] - total[:, inside]
                    o_new[a, b, rs, mine] = value
                    e_new[a, b, rs, slice(H + mine.start, H + mine.stop)] = value.astype(BF16)
            r0 += rows

    by_column(run, arrived[0::2], arrived[1::2])


def finish_kernel(mz, rimz, oz, inz, outz, mc, rimc, oc, inc, outc, out):
    def run(left, right):
        for k, (m, rim, o) in enumerate(((mz, rimz, oz), (mc, rimc, oc))):
            at = pl.ds(own(k), H)
            for a, b in PLANES:
                for side, other in ((0, left[k]), (1, right[k])):
                    cols = slice(H + H * side, 2 * H + H * side)
                    mine = slice(H * side, H * side + H)
                    total = m[a, b, :, cols] + rim[a, b, :, cols].astype(F32) + other[a, b].astype(F32)
                    out[a, b, at, mine] = o[a, b, :, mine] - RATE * total

    by_column(run, (inz, inc), (outz, outc))


def swapped(value, axis, first):
    pairs = [(i, i + 1) for i in range(first, lax.axis_size(axis) - 1, 2)]
    return lax.ppermute(value, axis, pairs + [(j, i) for i, j in pairs])


def sideways(inner, outer):
    return swapped(inner, "col", 0), swapped(outer, "col", 1)


def program(obj, probe, positions, counts, amplitudes):
    amps = amplitudes.reshape(6, N, N)
    strip, cut, band, half = (2, 2, H, 512), (2, 2, H, H), (2, 2, H, N), (2, 2, H, N)
    few, rest = (2, 2, FEW, N), (2, 2, H - FEW, N)

    iz, oz, ic, oc = local(edges_kernel, [(cut, BF16)] * 4, [VM])(obj)
    hi, ho = sideways(iz, oz)
    gi, go = sideways(ic, oc)
    base, scalars = local(setup_kernel, [((4, N, N), BF16), ((13,), jnp.int32)], [VM, SM, SM],
                          places=[VM, SM])(jnp.asarray(tables()), positions, counts)
    (ez,) = local(functools.partial(join_kernel, 0), [(strip, BF16)], [VM] * 3)(obj, hi, ho)
    hz = swapped(ez, "row", 1)
    (ec,) = local(functools.partial(join_kernel, 1), [(strip, BF16)], [VM] * 3)(obj, gi, go)
    hc = swapped(ec, "row", 0)
    rim_z, rim_c, mz, mc = slots(scalars, ez, ec, hz, hc, probe, amps, base)

    in_c = swapped(rim_c, "row", 0)
    in_z = swapped(rim_z, "row", 1)
    i1, o1, i2, o2 = local(functools.partial(bands_kernel, N), [(few, BF16)] * 2 + [(rest, BF16)] * 2, [VM] * 2)(mc, in_c)
    a1 = sideways(i1, o1)
    i0, o0 = local(functools.partial(bands_kernel, N), [(band, BF16)] * 2, [VM] * 2)(mz, in_z)
    a0 = sideways(i0, o0)
    a2 = sideways(i2, o2)
    ez2, oz = local(functools.partial(update_kernel, 0, 1), [(strip, BF16), (half, F32)], [VM] * 6)(
        mz, in_z, obj, ez, *a0)
    hz = swapped(ez2, "row", 1)
    ec2, oc = local(functools.partial(update_kernel, 1, 2), [(strip, BF16), (half, F32)], [VM] * 8)(
        mc, in_c, obj, ec, *a1, *a2)
    hc = swapped(ec2, "row", 0)
    rim_z, rim_c, mz, mc = slots(scalars, ez2, ec2, hz, hc, probe, amps, base)

    in_c = swapped(rim_c, "row", 0)
    in_z = swapped(rim_z, "row", 1)
    ic, oc_ = local(functools.partial(bands_kernel, H), [(cut, BF16)] * 2, [VM] * 2)(mc, in_c)
    ac = sideways(ic, oc_)
    iz, oz_ = local(functools.partial(bands_kernel, H), [(cut, BF16)] * 2, [VM] * 2)(mz, in_z)
    az = sideways(iz, oz_)
    (out,) = local(finish_kernel, [((2, 2, N, N), F32)], [VM] * 10)(
        mz, in_z, oz, *az, mc, in_c, oc, *ac)
    return out


def solution(mesh):
    return jax.shard_map(
        program,
        mesh=mesh,
        in_specs=(P(None, None, "row", "col"), P(), P("row", "col", None, None), P("row", "col"),
                  P("row", "col", None, None, None)),
        out_specs=P(None, None, "row", "col"),
        check_vma=False,
    )
```

time: 146 us -> 144 us (0.986)
  the two profiles are of different devices: /device:TPU:14 before, /device:TPU:12 now
where the time goes in v3:
time: 144 us; the launch traced here: 143 us
  starting transfers between devices  79.7 us (55%)
  waiting for transfers between devices  43.3 us (30%)
  Pallas kernels  17.8 us (12%)
    ppermute x22, starting transfers between devices, swapped(): return lax.ppermute(value, axis, pairs + [(j, i) for i, j in pairs])  79.7 us
    ppermute x22, waiting for transfers between devices, swapped(): return lax.ppermute(value, axis, pairs + [(j, i) for i, j in pairs])  43.3 us
    pallas_call x2, Pallas kernels, slots(): local(functools.partial(slots_kernel, LM, RM, RC), [(s, BF16), (s, BF16),...  14.2 us
  transfers between devices with their start and end apart: 22, of which 9 were waited for; matrix products, arithmetic and copies ran while one was open for 0% of the time, Pallas kernels for 2%

profile of v3, /device:TPU:12, one launch (start us, length us, event | category | flops | bytes accessed | tf_op | source)
XLA Modules:
  0.0 143.3 jit_solution(4223677611219364502)
XLA Ops:
  2.6 2.6 %collective-permute-start.1 = (bf16[2,2,128,128]{3,2,1,0:T(8,128)(2,1)S(1)}, bf16[2,2,128,128]{3,2,1,0:T(8,128)(2,1)S(1)}, u32[]{:S(2)}, u32[]{:S(2)}) collective-permute-start(bf16[2,2,128,128]{3,2,1,0:T(8,128)(2,1)S(1)} %get-tuple-element.35), channel_id=1, source_target_pairs={{1,2},{3,4},{5,6},{2,1},{4,3},{6,5},{9,10},{11,12},{13,14},{10,9},... | collective-permute-start | bytes 393224 | tf_op jit(solution)/shard_map/ppermute | solution.py:295
  5.2 2.4 %collective-permute-start.2 = (bf16[2,2,128,128]{3,2,1,0:T(8,128)(2,1)S(1)}, bf16[2,2,128,128]{3,2,1,0:T(8,128)(2,1)S(1)}, u32[]{:S(2)}, u32[]{:S(2)}) collective-permute-start(bf16[2,2,128,128]{3,2,1,0:T(8,128)(2,1)S(1)} %get-tuple-element.36), channel_id=1, source_target_pairs={{0,1},{2,3},{4,5},{6,7},{1,0},{3,2},{5,4},{7,6},{8,9},{10,11},{12,... | collective-permute-start | bytes 393224 | tf_op jit(solution)/shard_map/ppermute | solution.py:295
  11.8 4.7 %collective-permute-start.4 = (bf16[2,2,128,512]{3,2,1,0:T(8,128)(2,1)S(1)}, bf16[2,2,128,512]{3,2,1,0:T(8,128)(2,1)S(1)}, u32[]{:S(2)}, u32[]{:S(2)}) collective-permute-start(bf16[2,2,128,512]{3,2,1,0:T(8,128)(2,1)S(1)} %shard_map.66.ez.e), channel_id=1, source_target_pairs={{8,16},{24,32},{40,48},{56,64},{72,80},{88,96},{104,112},{120,128}... | collective-permute-start | bytes 1572872 | tf_op jit(solution)/shard_map/ppermute | solution.py:295
  18.8 7.2 %collective-permute-done.4.hz = bf16[2,2,128,512]{3,2,1,0:T(8,128)(2,1)S(1)} collective-permute-done((bf16[2,2,128,512]{3,2,1,0:T(8,128)(2,1)S(1)}, bf16[2,2,128,512]{3,2,1,0:T(8,128)(2,1)S(1)}, u32[]{:S(2)}, u32[]{:S(2)}) %collective-permute-start.4) | collective-permute-done | bytes 524320 | tf_op jit(solution)/shard_map/ppermute | solution.py:295
  26.1 7.3 %shard_map.68 = (bf16[2,2,128,512]{3,2,1,0:T(8,128)(2,1)S(1)}, bf16[2,2,128,512]{3,2,1,0:T(8,128)(2,1)S(1)}, f32[2,2,128,512]{3,2,1,0:T(8,128)S(1)}, f32[2,2,128,512]{3,2,1,0:T(8,128)S(1)}) custom-call(s32[13]{0:T(128)S(1)} %get-tuple-element.33.scalars, bf16[2,2,128,512]{3,2,1,0:T(8,128)(2,1)S(1)} %shard_map.66.ez.e, ...), custom_call_target="tpu_custom_call" | custom-call | flops 8589934592 | bytes 1048576 | tf_op jit(solution)/shard_map/pallas_call | solution.py:188
  33.3 4.6 %collective-permute-start.6 = (bf16[2,2,128,512]{3,2,1,0:T(8,128)(2,1)S(1)}, bf16[2,2,128,512]{3,2,1,0:T(8,128)(2,1)S(1)}, u32[]{:S(2)}, u32[]{:S(2)}) collective-permute-start(bf16[2,2,128,512]{3,2,1,0:T(8,128)(2,1)S(1)} %get-tuple-element.40), channel_id=1, source_target_pairs={{8,16},{24,32},{40,48},{56,64},{72,80},{88,96},{104,112},{120,128}... | collective-permute-start | bytes 1572872 | tf_op jit(solution)/shard_map/ppermute | solution.py:295
  37.9 6.0 %collective-permute-start.9 = (bf16[2,2,128,512]{3,2,1,0:T(8,128)(2,1)S(1)}, bf16[2,2,128,512]{3,2,1,0:T(8,128)(2,1)S(1)}, u32[]{:S(2)}, u32[]{:S(2)}) collective-permute-start(bf16[2,2,128,512]{3,2,1,0:T(8,128)(2,1)S(1)} %get-tuple-element.45), channel_id=1, source_target_pairs={{0,8},{16,24},{32,40},{48,56},{64,72},{80,88},{96,104},{112,120},{... | collective-permute-start | bytes 1572872 | tf_op jit(solution)/shard_map/ppermute | solution.py:295
  43.9 3.6 %collective-permute-done.6.rim = bf16[2,2,128,512]{3,2,1,0:T(8,128)(2,1)S(1)} collective-permute-done((bf16[2,2,128,512]{3,2,1,0:T(8,128)(2,1)S(1)}, bf16[2,2,128,512]{3,2,1,0:T(8,128)(2,1)S(1)}, u32[]{:S(2)}, u32[]{:S(2)}) %collective-permute-start.6) | collective-permute-done | bytes 524320 | tf_op jit(solution)/shard_map/ppermute | solution.py:295
  48.6 9.7 %collective-permute-start.8 = (bf16[2,2,128,256]{3,2,1,0:T(8,128)(2,1)S(1)}, bf16[2,2,128,256]{3,2,1,0:T(8,128)(2,1)S(1)}, u32[]{:S(2)}, u32[]{:S(2)}) collective-permute-start(bf16[2,2,128,256]{3,2,1,0:T(8,128)(2,1)S(1)} %get-tuple-element.42), channel_id=1, source_target_pairs={{1,2},{3,4},{5,6},{2,1},{4,3},{6,5},{9,10},{11,12},{13,14},{10,9},... | collective-permute-start | bytes 786440 | tf_op jit(solution)/shard_map/ppermute | solution.py:295
  58.5 5.4 %collective-permute-start.12 = (bf16[2,2,96,256]{3,2,1,0:T(8,128)(2,1)S(1)}, bf16[2,2,96,256]{3,2,1,0:T(8,128)(2,1)S(1)}, u32[]{:S(2)}, u32[]{:S(2)}) collective-permute-start(bf16[2,2,96,256]{3,2,1,0:T(8,128)(2,1)S(1)} %get-tuple-element.48), channel_id=1, source_target_pairs={{0,1},{2,3},{4,5},{6,7},{1,0},{3,2},{5,4},{7,6},{8,9},{10,11},{12,... | collective-permute-start | bytes 589832 | tf_op jit(solution)/shard_map/ppermute | solution.py:295
  66.0 6.8 %collective-permute-done.10.rest_0_ = bf16[2,2,32,256]{3,2,1,0:T(8,128)(2,1)S(1)} collective-permute-done((bf16[2,2,32,256]{3,2,1,0:T(8,128)(2,1)S(1)}, bf16[2,2,32,256]{3,2,1,0:T(8,128)(2,1)S(1)}, u32[]{:S(2)}, u32[]{:S(2)}) %collective-permute-start.10) | collective-permute-done | bytes 65568 | tf_op jit(solution)/shard_map/ppermute | solution.py:295
  72.9 4.0 %collective-permute-start.11 = (bf16[2,2,32,256]{3,2,1,0:T(8,128)(2,1)S(1)}, bf16[2,2,32,256]{3,2,1,0:T(8,128)(2,1)S(1)}, u32[]{:S(2)}, u32[]{:S(2)}) collective-permute-start(bf16[2,2,32,256]{3,2,1,0:T(8,128)(2,1)S(1)} %get-tuple-element.47), channel_id=1, source_target_pairs={{1,2},{3,4},{5,6},{2,1},{4,3},{6,5},{9,10},{11,12},{13,14},{10,9},... | collective-permute-start | bytes 196616 | tf_op jit(solution)/shard_map/ppermute | solution.py:295
  76.8 3.1 %collective-permute-done.11.rest_1_ = bf16[2,2,32,256]{3,2,1,0:T(8,128)(2,1)S(1)} collective-permute-done((bf16[2,2,32,256]{3,2,1,0:T(8,128)(2,1)S(1)}, bf16[2,2,32,256]{3,2,1,0:T(8,128)(2,1)S(1)}, u32[]{:S(2)}, u32[]{:S(2)}) %collective-permute-start.11) | collective-permute-done | bytes 65568 | tf_op jit(solution)/shard_map/ppermute | solution.py:295
  80.7 4.7 %collective-permute-start.14 = (bf16[2,2,128,512]{3,2,1,0:T(8,128)(2,1)S(1)}, bf16[2,2,128,512]{3,2,1,0:T(8,128)(2,1)S(1)}, u32[]{:S(2)}, u32[]{:S(2)}) collective-permute-start(bf16[2,2,128,512]{3,2,1,0:T(8,128)(2,1)S(1)} %get-tuple-element.43.ez), channel_id=1, source_target_pairs={{8,16},{24,32},{40,48},{56,64},{72,80},{88,96},{104,112},{120,128}... | collective-permute-start | bytes 1572872 | tf_op jit(solution)/shard_map/ppermute | solution.py:295
  85.4 9.4 %collective-permute-done.14.hz = bf16[2,2,128,512]{3,2,1,0:T(8,128)(2,1)S(1)} collective-permute-done((bf16[2,2,128,512]{3,2,1,0:T(8,128)(2,1)S(1)}, bf16[2,2,128,512]{3,2,1,0:T(8,128)(2,1)S(1)}, u32[]{:S(2)}, u32[]{:S(2)}) %collective-permute-start.14) | collective-permute-done | bytes 524320 | tf_op jit(solution)/shard_map/ppermute | solution.py:295
  94.8 6.9 %shard_map.73 = (bf16[2,2,128,512]{3,2,1,0:T(8,128)(2,1)S(1)}, bf16[2,2,128,512]{3,2,1,0:T(8,128)(2,1)S(1)}, f32[2,2,128,512]{3,2,1,0:T(8,128)S(1)}, f32[2,2,128,512]{3,2,1,0:T(8,128)S(1)}) custom-call(s32[13]{0:T(128)S(1)} %get-tuple-element.33.scalars, bf16[2,2,128,512]{3,2,1,0:T(8,128)(2,1)S(1)} %get-tuple-element.43.ez, ...), custom_call_target="tpu_custom_call" | custom-call | flops 8589934592 | bytes 1048576 | tf_op jit(solution)/shard_map/pallas_call | solution.py:188
  101.7 4.7 %collective-permute-start.16 = (bf16[2,2,128,512]{3,2,1,0:T(8,128)(2,1)S(1)}, bf16[2,2,128,512]{3,2,1,0:T(8,128)(2,1)S(1)}, u32[]{:S(2)}, u32[]{:S(2)}) collective-permute-start(bf16[2,2,128,512]{3,2,1,0:T(8,128)(2,1)S(1)} %get-tuple-element.52), channel_id=1, source_target_pairs={{8,16},{24,32},{40,48},{56,64},{72,80},{88,96},{104,112},{120,128}... | collective-permute-start | bytes 1572872 | tf_op jit(solution)/shard_map/ppermute | solution.py:295
  106.4 4.3 %collective-permute-start.19 = (bf16[2,2,128,512]{3,2,1,0:T(8,128)(2,1)S(1)}, bf16[2,2,128,512]{3,2,1,0:T(8,128)(2,1)S(1)}, u32[]{:S(2)}, u32[]{:S(2)}) collective-permute-start(bf16[2,2,128,512]{3,2,1,0:T(8,128)(2,1)S(1)} %get-tuple-element.57), channel_id=1, source_target_pairs={{0,8},{16,24},{32,40},{48,56},{64,72},{80,88},{96,104},{112,120},{... | collective-permute-start | bytes 1572872 | tf_op jit(solution)/shard_map/ppermute | solution.py:295
  110.7 5.2 %collective-permute-done.16.rim.rimz = bf16[2,2,128,512]{3,2,1,0:T(8,128)(2,1)S(1)} collective-permute-done((bf16[2,2,128,512]{3,2,1,0:T(8,128)(2,1)S(1)}, bf16[2,2,128,512]{3,2,1,0:T(8,128)(2,1)S(1)}, u32[]{:S(2)}, u32[]{:S(2)}) %collective-permute-start.16) | collective-permute-done | bytes 524320 | tf_op jit(solution)/shard_map/ppermute | solution.py:295
  116.0 2.4 %collective-permute-start.17 = (bf16[2,2,128,128]{3,2,1,0:T(8,128)(2,1)S(1)}, bf16[2,2,128,128]{3,2,1,0:T(8,128)(2,1)S(1)}, u32[]{:S(2)}, u32[]{:S(2)}) collective-permute-start(bf16[2,2,128,128]{3,2,1,0:T(8,128)(2,1)S(1)} %get-tuple-element.54), channel_id=1, source_target_pairs={{0,1},{2,3},{4,5},{6,7},{1,0},{3,2},{5,4},{7,6},{8,9},{10,11},{12,... | collective-permute-start | bytes 393224 | tf_op jit(solution)/shard_map/ppermute | solution.py:295
  118.4 7.9 %collective-permute-start.18 = (bf16[2,2,128,128]{3,2,1,0:T(8,128)(2,1)S(1)}, bf16[2,2,128,128]{3,2,1,0:T(8,128)(2,1)S(1)}, u32[]{:S(2)}, u32[]{:S(2)}) collective-permute-start(bf16[2,2,128,128]{3,2,1,0:T(8,128)(2,1)S(1)} %get-tuple-element.55), channel_id=1, source_target_pairs={{1,2},{3,4},{5,6},{2,1},{4,3},{6,5},{9,10},{11,12},{13,14},{10,9},... | collective-permute-start | bytes 393224 | tf_op jit(solution)/shard_map/ppermute | solution.py:295
  126.4 7.9 %collective-permute-start.20 = (bf16[2,2,128,128]{3,2,1,0:T(8,128)(2,1)S(1)}, bf16[2,2,128,128]{3,2,1,0:T(8,128)(2,1)S(1)}, u32[]{:S(2)}, u32[]{:S(2)}) collective-permute-start(bf16[2,2,128,128]{3,2,1,0:T(8,128)(2,1)S(1)} %get-tuple-element.59), channel_id=1, source_target_pairs={{0,1},{2,3},{4,5},{6,7},{1,0},{3,2},{5,4},{7,6},{8,9},{10,11},{12,... | collective-permute-start | bytes 393224 | tf_op jit(solution)/shard_map/ppermute | solution.py:295
  136.2 2.2 %collective-permute-done.20.inc = bf16[2,2,128,128]{3,2,1,0:T(8,128)(2,1)S(1)} collective-permute-done((bf16[2,2,128,128]{3,2,1,0:T(8,128)(2,1)S(1)}, bf16[2,2,128,128]{3,2,1,0:T(8,128)(2,1)S(1)}, u32[]{:S(2)}, u32[]{:S(2)}) %collective-permute-start.20) | collective-permute-done | bytes 131104 | tf_op jit(solution)/shard_map/ppermute | solution.py:295
  138.4 3.6 %collective-permute-done.21.outc = bf16[2,2,128,128]{3,2,1,0:T(8,128)(2,1)S(1)} collective-permute-done((bf16[2,2,128,128]{3,2,1,0:T(8,128)(2,1)S(1)}, bf16[2,2,128,128]{3,2,1,0:T(8,128)(2,1)S(1)}, u32[]{:S(2)}, u32[]{:S(2)}) %collective-permute-start.21) | collective-permute-done | bytes 131104 | tf_op jit(solution)/shard_map/ppermute | solution.py:295
  (46 shorter events, 15.6 us)
Async XLA Ops:
  1.3 8.2 %collective-permute-start = (bf16[2,2,128,128]{3,2,1,0:T(8,128)(2,1)S(1)}, bf16[2,2,128,128]{3,2,1,0:T(8,128)(2,1)S(1)}, u32[]{:S(2)}, u32[]{:S(2)}) collective-permute-start(bf16[2,2,128,128]{3,2,1,0:T(8,128)(2,1)S(1)} %get-tuple-element.34), channel_id=1, source_target_pairs={{0,1},{2,3},{4,5},{6,7},{1,0},{3,2},{5,4},{7,6},{8,9},{10,11},{12,... | collective-permute-start | bytes 393224 | tf_op jit(solution)/shard_map/ppermute | solution.py:295
  2.6 9.1 %collective-permute-start.1 = (bf16[2,2,128,128]{3,2,1,0:T(8,128)(2,1)S(1)}, bf16[2,2,128,128]{3,2,1,0:T(8,128)(2,1)S(1)}, u32[]{:S(2)}, u32[]{:S(2)}) collective-permute-start(bf16[2,2,128,128]{3,2,1,0:T(8,128)(2,1)S(1)} %get-tuple-element.35), channel_id=1, source_target_pairs={{1,2},{3,4},{5,6},{2,1},{4,3},{6,5},{9,10},{11,12},{13,14},{10,9},... | collective-permute-start | bytes 393224 | tf_op jit(solution)/shard_map/ppermute | solution.py:295
  5.2 11.4 %collective-permute-start.2 = (bf16[2,2,128,128]{3,2,1,0:T(8,128)(2,1)S(1)}, bf16[2,2,128,128]{3,2,1,0:T(8,128)(2,1)S(1)}, u32[]{:S(2)}, u32[]{:S(2)}) collective-permute-start(bf16[2,2,128,128]{3,2,1,0:T(8,128)(2,1)S(1)} %get-tuple-element.36), channel_id=1, source_target_pairs={{0,1},{2,3},{4,5},{6,7},{1,0},{3,2},{5,4},{7,6},{8,9},{10,11},{12,... | collective-permute-start | bytes 393224 | tf_op jit(solution)/shard_map/ppermute | solution.py:295
  7.6 9.0 %collective-permute-start.3 = (bf16[2,2,128,128]{3,2,1,0:T(8,128)(2,1)S(1)}, bf16[2,2,128,128]{3,2,1,0:T(8,128)(2,1)S(1)}, u32[]{:S(2)}, u32[]{:S(2)}) collective-permute-start(bf16[2,2,128,128]{3,2,1,0:T(8,128)(2,1)S(1)} %get-tuple-element.37), channel_id=1, source_target_pairs={{1,2},{3,4},{5,6},{2,1},{4,3},{6,5},{9,10},{11,12},{13,14},{10,9},... | collective-permute-start | bytes 393224 | tf_op jit(solution)/shard_map/ppermute | solution.py:295
  11.8 14.3 %copy-start.3 = (bf16[1,1,6,256,256]{4,3,2,1,0:T(8,128)(2,1)S(1)}, bf16[1,1,6,256,256]{4,3,2,1,0:T(8,128)(2,1)}, u32[]{:S(2)}) copy-start(bf16[1,1,6,256,256]{4,3,2,1,0:T(8,128)(2,1)} %param.10) | copy-start | bytes 2359300
  11.8 14.2 %collective-permute-start.4 = (bf16[2,2,128,512]{3,2,1,0:T(8,128)(2,1)S(1)}, bf16[2,2,128,512]{3,2,1,0:T(8,128)(2,1)S(1)}, u32[]{:S(2)}, u32[]{:S(2)}) collective-permute-start(bf16[2,2,128,512]{3,2,1,0:T(8,128)(2,1)S(1)} %shard_map.66.ez.e), channel_id=1, source_target_pairs={{8,16},{24,32},{40,48},{56,64},{72,80},{88,96},{104,112},{120,128}... | collective-permute-start | bytes 1572872 | tf_op jit(solution)/shard_map/ppermute | solution.py:295
  16.7 9.3 %collective-permute-start.5 = (bf16[2,2,128,512]{3,2,1,0:T(8,128)(2,1)S(1)}, bf16[2,2,128,512]{3,2,1,0:T(8,128)(2,1)}, u32[]{:S(2)}, u32[]{:S(2)}) collective-permute-start(bf16[2,2,128,512]{3,2,1,0:T(8,128)(2,1)S(1)} %shard_map.67.ec.e), channel_id=1, source_target_pairs={{0,8},{16,24},{32,40},{48,56},{64,72},{80,88},{96,104},{112,120},{... | collective-permute-start | bytes 1572872 | tf_op jit(solution)/shard_map/ppermute | solution.py:295
  33.3 14.1 %collective-permute-start.6 = (bf16[2,2,128,512]{3,2,1,0:T(8,128)(2,1)S(1)}, bf16[2,2,128,512]{3,2,1,0:T(8,128)(2,1)S(1)}, u32[]{:S(2)}, u32[]{:S(2)}) collective-permute-start(bf16[2,2,128,512]{3,2,1,0:T(8,128)(2,1)S(1)} %get-tuple-element.40), channel_id=1, source_target_pairs={{8,16},{24,32},{40,48},{56,64},{72,80},{88,96},{104,112},{120,128}... | collective-permute-start | bytes 1572872 | tf_op jit(solution)/shard_map/ppermute | solution.py:295
  37.9 20.4 %collective-permute-start.9 = (bf16[2,2,128,512]{3,2,1,0:T(8,128)(2,1)S(1)}, bf16[2,2,128,512]{3,2,1,0:T(8,128)(2,1)S(1)}, u32[]{:S(2)}, u32[]{:S(2)}) collective-permute-start(bf16[2,2,128,512]{3,2,1,0:T(8,128)(2,1)S(1)} %get-tuple-element.45), channel_id=1, source_target_pairs={{0,8},{16,24},{32,40},{48,56},{64,72},{80,88},{96,104},{112,120},{... | collective-permute-start | bytes 1572872 | tf_op jit(solution)/shard_map/ppermute | solution.py:295
  47.6 32.3 %copy-start.1 = (f32[2,2,256,256]{3,2,1,0:T(8,128)S(1)}, f32[2,2,256,256]{3,2,1,0:T(8,128)}, u32[]{:S(2)}) copy-start(f32[2,2,256,256]{3,2,1,0:T(8,128)} %obj.9) | copy-start | bytes 3145732
  47.6 32.7 %collective-permute-start.7 = (bf16[2,2,128,256]{3,2,1,0:T(8,128)(2,1)S(1)}, bf16[2,2,128,256]{3,2,1,0:T(8,128)(2,1)S(1)}, u32[]{:S(2)}, u32[]{:S(2)}) collective-permute-start(bf16[2,2,128,256]{3,2,1,0:T(8,128)(2,1)S(1)} %get-tuple-element.41), channel_id=1, source_target_pairs={{0,1},{2,3},{4,5},{6,7},{1,0},{3,2},{5,4},{7,6},{8,9},{10,11},{12,... | collective-permute-start | bytes 786440 | tf_op jit(solution)/shard_map/ppermute | solution.py:295
  48.6 31.8 %collective-permute-start.8 = (bf16[2,2,128,256]{3,2,1,0:T(8,128)(2,1)S(1)}, bf16[2,2,128,256]{3,2,1,0:T(8,128)(2,1)S(1)}, u32[]{:S(2)}, u32[]{:S(2)}) collective-permute-start(bf16[2,2,128,256]{3,2,1,0:T(8,128)(2,1)S(1)} %get-tuple-element.42), channel_id=1, source_target_pairs={{1,2},{3,4},{5,6},{2,1},{4,3},{6,5},{9,10},{11,12},{13,14},{10,9},... | collective-permute-start | bytes 786440 | tf_op jit(solution)/shard_map/ppermute | solution.py:295
  58.5 21.4 %collective-permute-start.12 = (bf16[2,2,96,256]{3,2,1,0:T(8,128)(2,1)S(1)}, bf16[2,2,96,256]{3,2,1,0:T(8,128)(2,1)S(1)}, u32[]{:S(2)}, u32[]{:S(2)}) collective-permute-start(bf16[2,2,96,256]{3,2,1,0:T(8,128)(2,1)S(1)} %get-tuple-element.48), channel_id=1, source_target_pairs={{0,1},{2,3},{4,5},{6,7},{1,0},{3,2},{5,4},{7,6},{8,9},{10,11},{12,... | collective-permute-start | bytes 589832 | tf_op jit(solution)/shard_map/ppermute | solution.py:295
  63.8 16.1 %collective-permute-start.13 = (bf16[2,2,96,256]{3,2,1,0:T(8,128)(2,1)S(1)}, bf16[2,2,96,256]{3,2,1,0:T(8,128)(2,1)S(1)}, u32[]{:S(2)}, u32[]{:S(2)}) collective-permute-start(bf16[2,2,96,256]{3,2,1,0:T(8,128)(2,1)S(1)} %get-tuple-element.49), channel_id=1, source_target_pairs={{1,2},{3,4},{5,6},{2,1},{4,3},{6,5},{9,10},{11,12},{13,14},{10,9},... | collective-permute-start | bytes 589832 | tf_op jit(solution)/shard_map/ppermute | solution.py:295
  65.8 7.1 %collective-permute-start.10 = (bf16[2,2,32,256]{3,2,1,0:T(8,128)(2,1)S(1)}, bf16[2,2,32,256]{3,2,1,0:T(8,128)(2,1)S(1)}, u32[]{:S(2)}, u32[]{:S(2)}) collective-permute-start(bf16[2,2,32,256]{3,2,1,0:T(8,128)(2,1)S(1)} %get-tuple-element.46), channel_id=1, source_target_pairs={{0,1},{2,3},{4,5},{6,7},{1,0},{3,2},{5,4},{7,6},{8,9},{10,11},{12,... | collective-permute-start | bytes 196616 | tf_op jit(solution)/shard_map/ppermute | solution.py:295
  72.9 7.0 %collective-permute-start.11 = (bf16[2,2,32,256]{3,2,1,0:T(8,128)(2,1)S(1)}, bf16[2,2,32,256]{3,2,1,0:T(8,128)(2,1)S(1)}, u32[]{:S(2)}, u32[]{:S(2)}) collective-permute-start(bf16[2,2,32,256]{3,2,1,0:T(8,128)(2,1)S(1)} %get-tuple-element.47), channel_id=1, source_target_pairs={{1,2},{3,4},{5,6},{2,1},{4,3},{6,5},{9,10},{11,12},{13,14},{10,9},... | collective-permute-start | bytes 196616 | tf_op jit(solution)/shard_map/ppermute | solution.py:295
  80.2 5.2 %collective-permute-start.15 = (bf16[2,2,128,512]{3,2,1,0:T(8,128)(2,1)S(1)}, bf16[2,2,128,512]{3,2,1,0:T(8,128)(2,1)S(1)}, u32[]{:S(2)}, u32[]{:S(2)}) collective-permute-start(bf16[2,2,128,512]{3,2,1,0:T(8,128)(2,1)S(1)} %get-tuple-element.50.ec), channel_id=1, source_target_pairs={{0,8},{16,24},{32,40},{48,56},{64,72},{80,88},{96,104},{112,120},{... | collective-permute-start | bytes 1572872 | tf_op jit(solution)/shard_map/ppermute | solution.py:295
  80.7 14.1 %collective-permute-start.14 = (bf16[2,2,128,512]{3,2,1,0:T(8,128)(2,1)S(1)}, bf16[2,2,128,512]{3,2,1,0:T(8,128)(2,1)S(1)}, u32[]{:S(2)}, u32[]{:S(2)}) collective-permute-start(bf16[2,2,128,512]{3,2,1,0:T(8,128)(2,1)S(1)} %get-tuple-element.43.ez), channel_id=1, source_target_pairs={{8,16},{24,32},{40,48},{56,64},{72,80},{88,96},{104,112},{120,128}... | collective-permute-start | bytes 1572872 | tf_op jit(solution)/shard_map/ppermute | solution.py:295
  101.7 14.2 %collective-permute-start.16 = (bf16[2,2,128,512]{3,2,1,0:T(8,128)(2,1)S(1)}, bf16[2,2,128,512]{3,2,1,0:T(8,128)(2,1)S(1)}, u32[]{:S(2)}, u32[]{:S(2)}) collective-permute-start(bf16[2,2,128,512]{3,2,1,0:T(8,128)(2,1)S(1)} %get-tuple-element.52), channel_id=1, source_target_pairs={{8,16},{24,32},{40,48},{56,64},{72,80},{88,96},{104,112},{120,128}... | collective-permute-start | bytes 1572872 | tf_op jit(solution)/shard_map/ppermute | solution.py:295
  106.4 19.9 %collective-permute-start.19 = (bf16[2,2,128,512]{3,2,1,0:T(8,128)(2,1)S(1)}, bf16[2,2,128,512]{3,2,1,0:T(8,128)(2,1)S(1)}, u32[]{:S(2)}, u32[]{:S(2)}) collective-permute-start(bf16[2,2,128,512]{3,2,1,0:T(8,128)(2,1)S(1)} %get-tuple-element.57), channel_id=1, source_target_pairs={{0,8},{16,24},{32,40},{48,56},{64,72},{80,88},{96,104},{112,120},{... | collective-permute-start | bytes 1572872 | tf_op jit(solution)/shard_map/ppermute | solution.py:295
  116.0 20.2 %collective-permute-start.17 = (bf16[2,2,128,128]{3,2,1,0:T(8,128)(2,1)S(1)}, bf16[2,2,128,128]{3,2,1,0:T(8,128)(2,1)S(1)}, u32[]{:S(2)}, u32[]{:S(2)}) collective-permute-start(bf16[2,2,128,128]{3,2,1,0:T(8,128)(2,1)S(1)} %get-tuple-element.54), channel_id=1, source_target_pairs={{0,1},{2,3},{4,5},{6,7},{1,0},{3,2},{5,4},{7,6},{8,9},{10,11},{12,... | collective-permute-start | bytes 393224 | tf_op jit(solution)/shard_map/ppermute | solution.py:295
  118.4 17.8 %collective-permute-start.18 = (bf16[2,2,128,128]{3,2,1,0:T(8,128)(2,1)S(1)}, bf16[2,2,128,128]{3,2,1,0:T(8,128)(2,1)S(1)}, u32[]{:S(2)}, u32[]{:S(2)}) collective-permute-start(bf16[2,2,128,128]{3,2,1,0:T(8,128)(2,1)S(1)} %get-tuple-element.55), channel_id=1, source_target_pairs={{1,2},{3,4},{5,6},{2,1},{4,3},{6,5},{9,10},{11,12},{13,14},{10,9},... | collective-permute-start | bytes 393224 | tf_op jit(solution)/shard_map/ppermute | solution.py:295
  126.4 12.0 %collective-permute-start.20 = (bf16[2,2,128,128]{3,2,1,0:T(8,128)(2,1)S(1)}, bf16[2,2,128,128]{3,2,1,0:T(8,128)(2,1)S(1)}, u32[]{:S(2)}, u32[]{:S(2)}) collective-permute-start(bf16[2,2,128,128]{3,2,1,0:T(8,128)(2,1)S(1)} %get-tuple-element.59), channel_id=1, source_target_pairs={{0,1},{2,3},{4,5},{6,7},{1,0},{3,2},{5,4},{7,6},{8,9},{10,11},{12,... | collective-permute-start | bytes 393224 | tf_op jit(solution)/shard_map/ppermute | solution.py:295
  134.3 7.7 %collective-permute-start.21 = (bf16[2,2,128,128]{3,2,1,0:T(8,128)(2,1)S(1)}, bf16[2,2,128,128]{3,2,1,0:T(8,128)(2,1)S(1)}, u32[]{:S(2)}, u32[]{:S(2)}) collective-permute-start(bf16[2,2,128,128]{3,2,1,0:T(8,128)(2,1)S(1)} %get-tuple-element.60), channel_id=1, source_target_pairs={{1,2},{3,4},{5,6},{2,1},{4,3},{6,5},{9,10},{11,12},{13,14},{10,9},... | collective-permute-start | bytes 393224 | tf_op jit(solution)/shard_map/ppermute | solution.py:295
  (4 other events, 17.3 us)
